TPU v7x, 256 devices: a whole 4x4x8 slice. The times are simulated.
256 devices in a mesh: gx: 4 (over x_lo, core), gy: 16 (over x_hi, z), gz: 4 (over y).
Axes of the slice: x: 4 (x_hi: 2, x_lo: 2; x = x_hi * 2 + x_lo), y: 4, z: 8, core: 2. Of those that a mesh axis runs over, the one named last changes fastest.
Arguments:
- field: bfloat16 [64, 8, 384, 1536], P(None, 'gz', 'gy', 'gx'), may hold values from -200 to 200, as said below
- mode_one_factor: bfloat16 [1536, 256], P('gx'), may hold values from -0.15625 to 0.15625
- mode_two_factor: bfloat16 [384, 256], P('gy'), may hold values from -0.3125 to 0.3125
Outputs:
- gram_one: float32 [1536, 1536], P('gx')
- gram_two: float32 [384, 384], P('gy')
- core: bfloat16 [64, 8, 256, 256], P('gx', 'gz', 'gy')
Inputs may be any that keep to these rules, and one draw needn't show every extreme that they name: `field`: the snapshot's values lie within -200 and 200.
All inputs are finite; a program needn't handle non-finite values.
Results may differ from a plain program's by a relative error of at most 0.005.
Values may be sent and summed in bfloat16 or wider, within the bound.
A program may use at most 128 MiB of HBM per device.

v0:
```python
import jax
import jax.numpy as jnp
from jax import lax
from jax.sharding import PartitionSpec as P


def local(field, mode_one_factor, mode_two_factor):
    vars_all, cells_three, cells_two, cells_one = field.shape
    rank_one = mode_one_factor.shape[1]
    count_gx = lax.axis_size("gx")
    own_rows = vars_all // count_gx
    total_three = cells_three * lax.axis_size("gz")
    total_two = cells_two * lax.axis_size("gy")
    flat_own = field.reshape(-1, cells_one)
    piece = lax.all_gather(field, "gx", axis=3, tiled=True)
    width = piece.shape[3]
    gram_block = lax.dot_general(
        flat_own,
        piece.reshape(-1, width),
        (((0,), (0,)), ((), ())),
        preferred_element_type=jnp.float32,
    )
    product = jnp.dot(
        field.reshape(-1, cells_one), mode_one_factor, preferred_element_type=jnp.float32
    )
    shrunk_sum = lax.psum_scatter(
        product.reshape(own_rows * lax.axis_size("gx"), cells_three, cells_two, rank_one),
        "gx",
        scatter_dimension=0,
        tiled=True,
    )
    gram_one = lax.psum(gram_block, ("gy", "gz")) * (1.0 / (vars_all * total_three * total_two))
    shrunk = shrunk_sum.astype(jnp.bfloat16)
    gram_two_block = jnp.einsum(
        "akjr,akqr->jq",
        shrunk,
        lax.all_gather(shrunk, "gy", axis=2, tiled=True),
        preferred_element_type=jnp.float32,
    )
    partial_core = jnp.einsum(
        "akjr,js->aksr", shrunk, mode_two_factor, preferred_element_type=jnp.float32
    )
    core = lax.psum_scatter(partial_core, "gy", scatter_dimension=2, tiled=True).astype(
        jnp.bfloat16
    )
    gram_two = lax.psum(gram_two_block, ("gx", "gz")) * (1.0 / (vars_all * total_three * rank_one))
    return (gram_one, gram_two, core)


def solution(mesh):
    placed = (P(None, "gz", "gy", "gx"), P("gx", None), P("gy", None))
    return jax.shard_map(
        local,
        mesh=mesh,
        in_specs=placed,
        out_specs=(P("gx", None), P("gy", None), P("gx", "gz", "gy", None)),
        check_vma=False,
    )
```

profile of v0, /device:TPU:8, one launch (start us, length us, event | category | flops | bytes accessed | tf_op | source)
XLA Modules:
  0.0 1197.3 jit_solution(16504379202459117194)
XLA Ops:
  7.2 0.0 copy-start
  7.2 0.0 all-gather.3.cloned.1.call-start
  7.2 3.7 copy.9
  10.9 0.0 copy-start.1
  10.9 0.0 all-gather.3.cloned.1.call-update
  10.9 0.0 reduce-scatter.3.cloned.1.call-start
  11.0 0.0 copy-done
  11.0 1.6 copy-done.1
  12.6 2.6 fusion.5
  15.2 0.0 reduce-scatter.3.cloned.1.call-update
  15.2 0.0 all-reduce.2.cloned.1.call-start
  15.3 89.8 %all-gather.3.cloned.1.call-done = bf16[64,2,24,1536]{3,0,2,1:T(8,128)(2,1)} async-done(((bf16[64,2,24,384]{3,0,2,1:T(8,128)(2,1)}), bf16[64,2,24,1536]{3,0,2,1:T(8,128)(2,1)}) %all-gather.3.cloned.1.call-update) | async-done | bytes 9437200 | tf_op jit(solution)/shard_map/all_gather | solution.py:15
  105.1 17.4 %fusion.2 = f32[384,1536]{1,0:T(8,128)} fusion(bf16[64,2,24,384]{3,2,1,0:T(8,128)(2,1)S(1)} %copy-done.1, bf16[64,2,24,1536]{3,0,2,1:T(8,128)(2,1)} %all-gather.3.cloned.1.call-done), kind=kOutput, calls=%fused_computation.3 | convolution fusion | flops 3623878656 | bytes 14155776 | tf_op jit(solution)/shard_map/dot_general | solution.py:17
  122.5 0.0 copy-start.3
  122.5 0.0 all-reduce.2.cloned.1.call-update
  122.5 0.0 all-gather.5.cloned.1.call-start
  122.5 26.8 %reduce-scatter.3.cloned.1.call-done = f32[16,2,24,256]{3,2,1,0:T(8,128)} async-done(((f32[64,2,24,256]{3,2,1,0:T(8,128)}), f32[16,2,24,256]{3,2,1,0:T(8,128)}) %reduce-scatter.3.cloned.1.call-update) | async-done | bytes 786448 | tf_op jit(solution)/shard_map/reduce_scatter | solution.py:26
  149.3 2.0 convert_element_type.6
  151.3 0.0 all-gather.5.cloned.1.call-update
  151.3 0.0 reduce-scatter.5.cloned.1.call-start
  151.3 0.0 copy-done.3
  151.4 5.5 convolution_bitcast_fusion
  156.9 10.5 copy.11
  167.4 0.0 reduce-scatter.5.cloned.1.call-update
  167.4 0.0 copy-start.2
  167.4 677.4 %all-reduce.2.cloned.1.call-done = f32[384,1536]{1,0:T(8,128)} async-done(((f32[384,1536]{1,0:T(8,128)}), f32[384,1536]{1,0:T(8,128)}) %all-reduce.2.cloned.1.call-update) | async-done | bytes 2359312 | tf_op jit(solution)/shard_map/psum | solution.py:32
  844.8 3.3 broadcast_multiply_fusion
  848.1 114.3 %all-gather.5.cloned.1.call-done = bf16[16,2,384,256]{3,2,1,0:T(8,128)(2,1)} async-done(((bf16[16,2,24,256]{3,2,1,0:T(8,128)(2,1)}), bf16[16,2,384,256]{3,2,1,0:T(8,128)(2,1)}) %all-gather.5.cloned.1.call-update) | async-done | bytes 6291472 | tf_op jit(solution)/shard_map/all_gather | solution.py:37
  962.4 0.0 copy-done.2
  962.4 4.5 convolution_bitcast_fusion.1
  966.9 52.5 %psum.15 = f32[24,384]{1,0:T(8,128)S(1)} all-reduce(f32[24,384]{1,0:T(8,128)S(1)} %convolution_bitcast_fusion.1), channel_id=1, replica_groups=mesh['gx'=4,'gy'=16,'gz'=4] {'gx','gz'}, use_global_device_ids=true, to_apply=%region_2.0 | all-reduce | flops 9216 | bytes 73728 | tf_op jit(solution)/shard_map/psum | solution.py:46
  1019.4 0.6 broadcast_multiply_fusion.1
  1020.0 168.8 %reduce-scatter.5.cloned.1.call-done = f32[16,2,16,256]{3,0,1,2:T(8,128)} async-done(((f32[16,2,256,256]{3,0,1,2:T(8,128)}), f32[16,2,16,256]{3,0,1,2:T(8,128)}) %reduce-scatter.5.cloned.1.call-update) | async-done | bytes 524304 | tf_op jit(solution)/shard_map/reduce_scatter | solution.py:43
  1188.8 1.1 convert_element_type.7
  1189.9 0.9 copy.12
Async XLA Ops:
  7.2 3.8 copy-start
  7.2 97.9 %all-gather.3.cloned.1.call-start = ((), (), s32[]{:S(2)}) async-start(), calls=%async_computation.2 | async-start | bytes 11796480 | tf_op jit(solution)/shard_map/all_gather | solution.py:15
  10.9 1.7 copy-start.1
  10.9 138.4 %reduce-scatter.3.cloned.1.call-start = ((), (), s32[]{:S(2)}) async-start(), calls=%async_computation.4 | async-start | bytes 3932160 | tf_op jit(solution)/shard_map/reduce_scatter | solution.py:26
  15.2 829.6 %all-reduce.2.cloned.1.call-start = ((), (), s32[]{:S(2)}) async-start(), calls=%async_computation.3 | async-start | bytes 4718592 | tf_op jit(solution)/shard_map/psum | solution.py:32
  122.5 28.9 %copy-start.3 = (bf16[24,256]{1,0:T(8,128)(2,1)S(1)}, bf16[24,256]{1,0:T(8,128)(2,1)}, u32[]{:S(2)}) copy-start(bf16[24,256]{1,0:T(8,128)(2,1)} %param.5) | copy-start | bytes 36868
  122.5 839.9 %all-gather.5.cloned.1.call-start = ((), (), s32[]{:S(2)}) async-start(), calls=%async_computation.5 | async-start | bytes 6684672 | tf_op jit(solution)/shard_map/all_gather | solution.py:37
  151.3 1037.5 %reduce-scatter.5.cloned.1.call-start = ((), (), s32[]{:S(2)}) async-start(), calls=%async_computation.6 | async-start | bytes 8912896 | tf_op jit(solution)/shard_map/reduce_scatter | solution.py:43
  167.4 795.0 %copy-start.2 = (bf16[16,2,24,256]{3,2,1,0:T(8,128)(2,1)S(1)}, bf16[16,2,24,256]{3,2,1,0:T(8,128)(2,1)}, u32[]{:S(2)}) copy-start(bf16[16,2,24,256]{3,2,1,0:T(8,128)(2,1)} %convert_element_type.6) | copy-start | bytes 1179652
Sparse Core Ops, SparseCore 0:
  11.1 93.9 all-gather.2
  107.6 41.6 reduce-scatter.2
  152.5 692.2 all-reduce.1
  847.3 115.0 all-gather.4
  966.3 222.4 reduce-scatter.4
where the time goes:
time: 1200 us
  waiting for transfers between devices  1080 us (90%)
  blocking collectives  52.5 us (4%)
  matrix products  30.1 us (3%)
  local copies, waits for them, and re-layouts  16.6 us (1%)
  between operations  13.8 us (1%)
    psum x1, waiting for transfers between devices, local(): lax.psum(gram_block, ('gy', 'gz'))  677 us
    reduce_scatter x1, waiting for transfers between devices, local(): lax.psum_scatter(partial_core, 'gy', scatter_dimension=2, tiled=True)  169 us
    all_gather x1, waiting for transfers between devices, local(): lax.all_gather(shrunk, 'gy', axis=2, tiled=True)  114 us
    all_gather x1, waiting for transfers between devices, local(): piece = lax.all_gather(field, 'gx', axis=3, tiled=True)  89.8 us
    psum x1, blocking collectives, local(): lax.psum(gram_two_block, ('gx', 'gz'))  52.5 us
    reduce_scatter x1, waiting for transfers between devices, local(): lax.psum_scatter(product.reshape(own_rows * lax.axis_size('gx'), cells_th...  26.8 us
  transfers between devices with their start and end apart: 5, of which 5 were waited for; matrix products, arithmetic and copies ran while one was open for 4% of the time, Pallas kernels for 0%

commit v1 on v0

v1 whole, which is shorter than its diff:
```python
import jax
import jax.numpy as jnp
from jax import lax
from jax.sharding import PartitionSpec as P


def local(field, mode_one_factor, mode_two_factor):
    vars_all, cells_three, cells_two, cells_one = field.shape
    count_gx = lax.axis_size("gx")
    count_gy = lax.axis_size("gy")
    own_rows = vars_all // count_gx
    total_three = cells_three * lax.axis_size("gz")
    total_two = cells_two * count_gy
    rank_one = mode_one_factor.shape[1]
    rank_two = mode_two_factor.shape[1]
    own_ranks = rank_two // count_gy

    factor_one = lax.all_gather(mode_one_factor, "gx", axis=0, tiled=True)
    piece = lax.all_gather(field, "gx", axis=3, tiled=True)
    width = piece.shape[3]
    gram_block = lax.dot_general(
        field.reshape(-1, cells_one),
        piece.reshape(-1, width),
        (((0,), (0,)), ((), ())),
        preferred_element_type=jnp.float32,
    )
    gram_sum = lax.psum(lax.psum(gram_block, "gz"), "gy")
    gram_one = gram_sum * (1.0 / (vars_all * total_three * total_two))

    own_vars = lax.dynamic_slice_in_dim(piece, lax.axis_index("gx") * own_rows, own_rows, axis=0)
    shrunk = jnp.dot(
        own_vars.reshape(-1, width), factor_one, preferred_element_type=jnp.float32
    ).astype(jnp.bfloat16).reshape(own_rows, cells_three, cells_two, rank_one)

    shrunk_all = lax.all_gather(shrunk, "gy", axis=2, tiled=True)
    gram_two_block = jnp.einsum(
        "akjr,akqr->jq", shrunk, shrunk_all, preferred_element_type=jnp.float32
    )
    gram_two = lax.psum(gram_two_block, ("gx", "gz")) * (1.0 / (vars_all * total_three * rank_one))

    factor_two = lax.all_gather(mode_two_factor, "gy", axis=0, tiled=True)
    own_cols = lax.dynamic_slice_in_dim(factor_two, lax.axis_index("gy") * own_ranks, own_ranks, axis=1)
    core = jnp.einsum(
        "akjr,js->aksr", shrunk_all, own_cols, preferred_element_type=jnp.float32
    ).astype(jnp.bfloat16)
    return (gram_one, gram_two, core)


def solution(mesh):
    placed = (P(None, "gz", "gy", "gx"), P("gx", None), P("gy", None))
    return jax.shard_map(
        local,
        mesh=mesh,
        in_specs=placed,
        out_specs=(P("gx", None), P("gy", None), P("gx", "gz", "gy", None)),
        check_vma=False,
    )
```

time: 1200 us -> 535 us (0.45)
  waiting for transfers between devices: 1080 us -> 392 us
  blocking collectives: 52.5 us -> 103 us
  local copies, waits for them, and re-layouts: 16.6 us -> 1.83 us
    psum x1 -> x2, waiting for transfers between devices: 677 us -> 183 us  [local(): gram_sum = lax.psum(lax.psum(gram_block, 'gz'), 'gy')]
    reduce_scatter x2 -> x0, waiting for transfers between devices: 196 us -> none  [the longest x1 169 us: local(): lax.psum_scatter(partial_core, 'gy', scatter_dimension=2, tiled=True)]
    all_gather x0 -> x2, blocking collectives: none -> 50.8 us  [the longest x1 42.2 us: local(): factor_two = lax.all_gather(mode_two_factor, 'gy', axis=0, tiled=True)]
  transfers between devices with their start and end apart: 5 -> 4, of which waited for: 5 -> 4; matrix products, arithmetic and copies ran while one was open for 4% -> 1% of each run, Pallas kernels for 0% -> 0%
where the time goes in v1:
time: 535 us; the launch traced here: 534 us
  waiting for transfers between devices  392 us (73%)
  blocking collectives  103 us (19%)
  matrix products  18.3 us (3%)
  between operations  13.8 us (3%)
    psum x2, waiting for transfers between devices, local(): gram_sum = lax.psum(lax.psum(gram_block, 'gz'), 'gy')  183 us
    all_gather x1, waiting for transfers between devices, local(): shrunk_all = lax.all_gather(shrunk, 'gy', axis=2, tiled=True)  113 us
    all_gather x1, waiting for transfers between devices, local(): piece = lax.all_gather(field, 'gx', axis=3, tiled=True)  95.9 us
    psum x1, blocking collectives, local(): lax.psum(gram_two_block, ('gx', 'gz'))  52.4 us
    all_gather x1, blocking collectives, local(): factor_two = lax.all_gather(mode_two_factor, 'gy', axis=0, tiled=True)  42.2 us
  transfers between devices with their start and end apart: 4, of which 4 were waited for; matrix products, arithmetic and copies ran while one was open for 1% of the time, Pallas kernels for 0%

profile of v1, /device:TPU:8, one launch (start us, length us, event | category | flops | bytes accessed | tf_op | source)
XLA Modules:
  0.0 533.7 jit_solution(3255514334234658207)
XLA Ops:
  7.2 0.0 copy-start
  7.2 0.0 all-gather.3.cloned.1.call-start
  7.2 0.7 all-gather.3.cloned.1.call-update
  7.9 0.0 all-reduce.3.cloned.1.call-start
  8.0 95.9 %all-gather.3.cloned.1.call-done = bf16[64,2,24,1536]{3,2,1,0:T(8,128)(2,1)} async-done(((bf16[64,2,24,384]{3,2,1,0:T(8,128)(2,1)}), bf16[64,2,24,1536]{3,2,1,0:T(8,128)(2,1)}) %all-gather.3.cloned.1.call-update) | async-done | bytes 9437200 | tf_op jit(solution)/shard_map/all_gather | solution.py:19
  103.8 0.0 copy-done
  103.8 7.8 %convolution_bitcast_fusion = f32[384,1536]{1,0:T(8,128)} fusion(bf16[64,2,24,384]{3,2,1,0:T(8,128)(2,1)S(1)} %copy-done, bf16[64,2,24,1536]{3,2,1,0:T(8,128)(2,1)} %all-gather.3.cloned.1.call-done), kind=kOutput, calls=%fused_computation | convolution fusion | flops 3623878656 | bytes 14155776 | tf_op jit(solution)/shard_map/dot_general | solution.py:21
  111.6 0.0 copy-start.2
  111.6 0.0 all-reduce.3.cloned.1.call-update
  111.6 0.0 all-reduce.5.cloned.1.call-start
  111.7 69.5 %all-reduce.3.cloned.1.call-done = f32[384,1536]{1,0:T(8,128)} async-done(((f32[384,1536]{1,0:T(8,128)}), f32[384,1536]{1,0:T(8,128)}) %all-reduce.3.cloned.1.call-update) | async-done | bytes 2359312 | tf_op jit(solution)/shard_map/psum | solution.py:27
  181.1 0.0 all-reduce.5.cloned.1.call-update
  181.2 0.0 all-gather.5.cloned.1.call-start
  181.2 0.0 copy-done.2
  181.2 8.6 %all_gather.13 = bf16[1536,256]{1,0:T(8,128)(2,1)S(1)} all-gather(bf16[384,256]{1,0:T(8,128)(2,1)S(1)} %copy-done.2), channel_id=1, replica_groups=mesh['gx'=4,'gy'=16,'gz'=4] {'gx'}, dimensions={0}, use_global_device_ids=true | all-gather | bytes 983040 | tf_op jit(solution)/shard_map/all_gather | solution.py:18
  189.8 1.8 constant_dynamic-slice_fusion
  191.6 0.0 copy-start.3
  191.6 1.5 convolution_convert_fusion
  193.2 0.0 all-gather.5.cloned.1.call-update
  193.2 0.0 copy-done.3
  193.2 42.2 %all_gather.15 = bf16[384,256]{1,0:T(8,128)(2,1)S(1)} all-gather(bf16[24,256]{1,0:T(8,128)(2,1)S(1)} %copy-done.3), channel_id=1, replica_groups=mesh['gx'=4,'gy'=16,'gz'=4] {'gy'}, dimensions={0}, use_global_device_ids=true | all-gather | bytes 208896 | tf_op jit(solution)/shard_map/all_gather | solution.py:41
  235.4 0.0 copy-start.1
  235.4 113.6 %all-reduce.5.cloned.1.call-done = f32[384,1536]{1,0:T(8,128)} async-done(((f32[384,1536]{1,0:T(8,128)}), f32[384,1536]{1,0:T(8,128)}) %all-reduce.5.cloned.1.call-update) | async-done | bytes 2359312 | tf_op jit(solution)/shard_map/psum | solution.py:27
  349.0 3.3 broadcast_multiply_fusion
  352.3 112.8 %all-gather.5.cloned.1.call-done = bf16[16,2,384,256]{3,2,1,0:T(8,128)(2,1)} async-done(((bf16[16,2,24,256]{3,2,1,0:T(8,128)(2,1)}), bf16[16,2,384,256]{3,2,1,0:T(8,128)(2,1)}) %all-gather.5.cloned.1.call-update) | async-done | bytes 6291472 | tf_op jit(solution)/shard_map/all_gather | solution.py:35
  465.1 0.0 copy-done.1
  465.1 4.5 convolution_bitcast_fusion.1
  469.6 52.4 %psum.23 = f32[24,384]{1,0:T(8,128)S(1)} all-reduce(f32[24,384]{1,0:T(8,128)S(1)} %convolution_bitcast_fusion.1), channel_id=1, replica_groups=mesh['gx'=4,'gy'=16,'gz'=4] {'gx','gz'}, use_global_device_ids=true, to_apply=%region_2.0 | all-reduce | flops 9216 | bytes 73728 | tf_op jit(solution)/shard_map/psum | solution.py:39
  522.0 0.6 broadcast_multiply_fusion.1
  522.6 4.5 fusion
Async XLA Ops:
  7.2 96.7 %copy-start = (bf16[64,2,24,384]{3,2,1,0:T(8,128)(2,1)S(1)}, bf16[64,2,24,384]{3,2,1,0:T(8,128)(2,1)}, u32[]{:S(2)}) copy-start(bf16[64,2,24,384]{3,2,1,0:T(8,128)(2,1)} %param.3) | copy-start | bytes 7077892
  7.2 96.6 %all-gather.3.cloned.1.call-start = ((), (), s32[]{:S(2)}) async-start(), calls=%async_computation | async-start | bytes 11796480 | tf_op jit(solution)/shard_map/all_gather | solution.py:19
  7.9 173.2 %all-reduce.3.cloned.1.call-start = ((), (), s32[]{:S(2)}) async-start(), calls=%async_computation.1 | async-start | bytes 4718592 | tf_op jit(solution)/shard_map/psum | solution.py:27
  111.6 69.6 %copy-start.2 = (bf16[384,256]{1,0:T(8,128)(2,1)S(1)}, bf16[384,256]{1,0:T(8,128)(2,1)}, u32[]{:S(2)}) copy-start(bf16[384,256]{1,0:T(8,128)(2,1)} %param.4) | copy-start | bytes 589828
  111.6 237.3 %all-reduce.5.cloned.1.call-start = ((), (), s32[]{:S(2)}) async-start(), calls=%async_computation.2 | async-start | bytes 4718592 | tf_op jit(solution)/shard_map/psum | solution.py:27
  181.2 283.9 %all-gather.5.cloned.1.call-start = ((), (), s32[]{:S(2)}) async-start(), calls=%async_computation.3 | async-start | bytes 6684672 | tf_op jit(solution)/shard_map/all_gather | solution.py:35
  191.6 1.6 copy-start.3
  235.4 229.6 %copy-start.1 = (bf16[768,256]{1,0:T(8,128)(2,1)S(1)}, bf16[768,256]{1,0:T(8,128)(2,1)}, u32[]{:S(2)}) copy-start(bf16[768,256]{1,0:T(8,128)(2,1)} %convolution_convert_fusion) | copy-start | bytes 1179652
Sparse Core Ops, SparseCore 0:
  9.8 93.9 all-gather.2
  111.8 69.3 all-reduce.2
  183.8 165.1 all-reduce.4
  351.5 113.5 all-gather.4

commit v2 on v1

--- a/solution.py
+++ b/solution.py
@@ -15,30 +15,50 @@
     rank_two = mode_two_factor.shape[1]
     own_ranks = rank_two // count_gy
 
-    factor_one = lax.all_gather(mode_one_factor, "gx", axis=0, tiled=True)
-    piece = lax.all_gather(field, "gx", axis=3, tiled=True)
+    slab = cells_three * cells_two
+    factor_slabs = -(-rank_one // slab)
+    factor_t = jnp.pad(mode_one_factor.T, ((0, factor_slabs * slab - rank_one), (0, 0)))
+    joined = jnp.concatenate(
+        [field, factor_t.reshape(factor_slabs, cells_three, cells_two, cells_one)], axis=0
+    )
+    joined_all = lax.all_gather(joined, "gx", axis=3, tiled=True)
+    piece = joined_all[:vars_all]
     width = piece.shape[3]
+    factor_one_t = joined_all[vars_all:].reshape(factor_slabs * slab, width)[:rank_one]
+
     gram_block = lax.dot_general(
         field.reshape(-1, cells_one),
         piece.reshape(-1, width),
         (((0,), (0,)), ((), ())),
         preferred_element_type=jnp.float32,
     )
+
+    own_vars = lax.dynamic_slice_in_dim(piece, lax.axis_index("gx") * own_rows, own_rows, axis=0)
+    shrunk = lax.dot_general(
+        own_vars.reshape(-1, width),
+        factor_one_t,
+        (((1,), (1,)), ((), ())),
+        preferred_element_type=jnp.float32,
+    ).astype(jnp.bfloat16).reshape(own_rows, cells_three, cells_two, rank_one)
+
+    if rank_one == rank_two:
+        extra = jnp.broadcast_to(mode_two_factor, (1, cells_three) + mode_two_factor.shape)
+        both_all = lax.all_gather(jnp.concatenate([shrunk, extra], axis=0), "gy", axis=2, tiled=True)
+        shrunk_all = both_all[:own_rows]
+        factor_two = both_all[own_rows, 0]
+    else:
+        shrunk_all = lax.all_gather(shrunk, "gy", axis=2, tiled=True)
+        factor_two = lax.all_gather(mode_two_factor, "gy", axis=0, tiled=True)
+
+    gram_block, shrunk_all, factor_two = lax.optimization_barrier((gram_block, shrunk_all, factor_two))
     gram_sum = lax.psum(lax.psum(gram_block, "gz"), "gy")
     gram_one = gram_sum * (1.0 / (vars_all * total_three * total_two))
 
-    own_vars = lax.dynamic_slice_in_dim(piece, lax.axis_index("gx") * own_rows, own_rows, axis=0)
-    shrunk = jnp.dot(
-        own_vars.reshape(-1, width), factor_one, preferred_element_type=jnp.float32
-    ).astype(jnp.bfloat16).reshape(own_rows, cells_three, cells_two, rank_one)
-
-    shrunk_all = lax.all_gather(shrunk, "gy", axis=2, tiled=True)
     gram_two_block = jnp.einsum(
         "akjr,akqr->jq", shrunk, shrunk_all, preferred_element_type=jnp.float32
     )
     gram_two = lax.psum(gram_two_block, ("gx", "gz")) * (1.0 / (vars_all * total_three * rank_one))
 
-    factor_two = lax.all_gather(mode_two_factor, "gy", axis=0, tiled=True)
     own_cols = lax.dynamic_slice_in_dim(factor_two, lax.axis_index("gy") * own_ranks, own_ranks, axis=1)
     core = jnp.einsum(
         "akjr,js->aksr", shrunk_all, own_cols, preferred_element_type=jnp.float32

time: 535 us -> 505 us (0.944)
  blocking collectives: 103 us -> 54.6 us
  local copies, waits for them, and re-layouts: 1.83 us -> 29.3 us
  waiting for transfers between devices: 392 us -> 376 us
  matrix products: 18.3 us -> 26.3 us
    all_gather x2 -> x0, blocking collectives: 50.8 us -> none  [the longest x1 42.2 us: local(): factor_two = lax.all_gather(mode_two_factor, 'gy', axis=0, tiled=True)]
    psum x2, waiting for transfers between devices: 183 us -> 160 us  [local(): gram_sum = lax.psum(lax.psum(gram_block, 'gz'), 'gy')]
    slice x0 -> x6, local copies, waits for them, and re-layouts: none -> 18.4 us  [the longest x1 8.34 us: local(): piece = joined_all[:vars_all]]
    all_gather x2, waiting for transfers between devices: 209 us -> 216 us  [the longest x1 112 us: local(): lax.all_gather(jnp.concatenate([shrunk, extra], axis=0), 'gy', axis=2, ti...]
    unnamed x8 -> x12, local copies, waits for them, and re-layouts: 0.02 us -> 6.62 us
  transfers between devices with their start and end apart: 4 -> 4, of which waited for: 4 -> 4; matrix products, arithmetic and copies ran while one was open for 1% -> 5% of each run, Pallas kernels for 0% -> 0%
where the time goes in v2:
time: 505 us
  waiting for transfers between devices  376 us (74%)
  blocking collectives  54.6 us (11%)
  local copies, waits for them, and re-layouts  29.3 us (6%)
  matrix products  26.3 us (5%)
  between operations  13.9 us (3%)
    psum x2, waiting for transfers between devices, local(): gram_sum = lax.psum(lax.psum(gram_block, 'gz'), 'gy')  160 us
    all_gather x1, waiting for transfers between devices, local(): lax.all_gather(jnp.concatenate([shrunk, extra], axis=0), 'gy', axis=2, ti...  112 us
    all_gather x1, waiting for transfers between devices, local(): joined_all = lax.all_gather(joined, 'gx', axis=3, tiled=True)  104 us
    psum x1, blocking collectives, local(): lax.psum(gram_two_block, ('gx', 'gz'))  54.6 us
  transfers between devices with their start and end apart: 4, of which 4 were waited for; matrix products, arithmetic and copies ran while one was open for 5% of the time, Pallas kernels for 0%

profile of v2, /device:TPU:8, one launch (start us, length us, event | category | flops | bytes accessed | tf_op | source)
XLA Modules:
  0.0 504.7 jit_solution(13145837295311710367)
XLA Ops:
  7.2 0.0 all-gather.3.cloned.1.call-start
  7.2 1.1 copy.24
  8.3 0.1 copy.26
  8.4 2.2 copy.25
  10.7 1.9 pad_maximum_fusion
  12.5 0.0 all-gather.3.cloned.1.call-update
  12.5 0.0 all-gather.5.cloned.1.call-start
  12.6 103.7 %all-gather.3.cloned.1.call-done = bf16[70,2,24,1536]{3,0,2,1:T(8,128)(2,1)} async-done(((bf16[70,2,24,384]{3,0,2,1:T(8,128)(2,1)}), bf16[70,2,24,1536]{3,0,2,1:T(8,128)(2,1)}) %all-gather.3.cloned.1.call-update) | async-done | bytes 10321936 | tf_op jit(solution)/shard_map/all_gather | solution.py:24
  116.3 0.0 slice-start
  116.3 1.3 slice-done
  117.6 0.3 copy.29
  117.9 8.3 %slice.20 = bf16[64,2,24,1536]{3,0,2,1:T(8,128)(2,1)} slice(bf16[70,2,24,1536]{3,0,2,1:T(8,128)(2,1)} %all-gather.3.cloned.1.call-done), slice={[0:64], [0:2], [0:24], [0:1536]} | slice | bytes 18874368 | tf_op jit(solution)/shard_map/slice | solution.py:25
  126.2 1.8 constant_dynamic-slice_fusion
  128.0 1.3 copy.28
  129.3 0.0 copy-start.3
  129.3 0.0 copy-start
  129.4 0.8 convolution_convert_fusion
  130.2 0.0 copy-done.3
  130.2 0.0 copy-start.1
  130.2 0.7 copy-done.1
  131.0 1.1 copy.30
  132.0 0.0 all-gather.5.cloned.1.call-update
  132.1 0.0 all-reduce.4.cloned.1.call-start
  132.1 0.0 copy-done
  132.1 9.1 %convolution_bitcast_fusion = f32[384,1536]{0,1:T(8,128)} fusion(bf16[64,2,24,384]{3,2,1,0:T(8,128)(2,1)S(1)} %copy-done, bf16[70,2,24,1536]{3,0,2,1:T(8,128)(2,1)} %all-gather.3.cloned.1.call-done), kind=kOutput, calls=%fused_computation.4 | convolution fusion | flops 3623878656 | bytes 14155776 | tf_op jit(solution)/shard_map/dot_general | solution.py:29
  141.2 112.4 %all-gather.5.cloned.1.call-done = bf16[17,2,384,256]{3,1,0,2:T(2,128)(2,1)} async-done(((bf16[17,2,24,256]{3,1,0,2:T(2,128)(2,1)}), bf16[17,2,384,256]{3,1,0,2:T(2,128)(2,1)}) %all-gather.5.cloned.1.call-update) | async-done | bytes 6684688 | tf_op jit(solution)/shard_map/all_gather | solution.py:46
  253.6 1.3 slice.24
  254.9 0.6 copy.38
  255.5 7.3 %slice.23 = bf16[16,2,384,256]{3,1,0,2:T(2,128)(2,1)} slice(bf16[17,2,384,256]{3,1,0,2:T(2,128)(2,1)} %all-gather.5.cloned.1.call-done), slice={[0:16], [0:2], [0:384], [0:256]} | slice | bytes 12582912 | tf_op jit(solution)/shard_map/slice | solution.py:47
  262.7 0.0 copy-start.2
  262.7 0.0 all-reduce.4.cloned.1.call-update
  262.8 0.2 all-reduce.6.cloned.1.call-start
  263.0 63.8 %all-reduce.4.cloned.1.call-done = f32[384,1536]{0,1:T(8,128)} async-done(((f32[384,1536]{0,1:T(8,128)}), f32[384,1536]{0,1:T(8,128)}) %all-reduce.4.cloned.1.call-update) | async-done | bytes 2359312 | tf_op jit(solution)/shard_map/psum | solution.py:54
  326.8 0.0 all-reduce.6.cloned.1.call-update
  326.8 0.0 copy-done.2
  326.8 9.5 %fusion.10 = f32[24,384]{1,0:T(8,128)S(1)} fusion(bf16[16,2,24,256]{3,2,1,0:T(8,128)(2,1)S(1)} %bitcast.30, bf16[16,2,384,256]{3,1,0,2:T(2,128)(2,1)} %slice.23), kind=kOutput, calls=%fused_computation.10 | convolution fusion | flops 150994944 | bytes 6721536 | tf_op jit(solution)/shard_map/akjr,akqr->jq/dot_general | solution.py:57
  336.3 54.6 %psum.23 = f32[24,384]{1,0:T(8,128)S(1)} all-reduce(f32[24,384]{1,0:T(8,128)S(1)} %fusion.10), channel_id=1, replica_groups=mesh['gx'=4,'gy'=16,'gz'=4] {'gx','gz'}, use_global_device_ids=true, to_apply=%region_2.3 | all-reduce | flops 9216 | bytes 73728 | tf_op jit(solution)/shard_map/psum | solution.py:60
  390.9 0.6 broadcast_multiply_fusion.1
  391.5 6.9 %fusion.7 = bf16[16,2,16,256]{3,2,1,0:T(8,128)(2,1)} fusion(bf16[16,2,384,256]{3,1,0,2:T(2,128)(2,1)} %slice.23, bf16[384,256]{0,1:T(8,128)(2,1)S(1)} %bitcast.31, s32[]{:T(128)S(6)} %select_n.7), kind=kOutput, calls=%fused_computation.9 | convolution fusion | flops 100794368 | bytes 6565892 | tf_op jit(solution)/shard_map/akjr,js->aksr/dot_general | solution.py:63
  398.4 95.9 %all-reduce.6.cloned.1.call-done = f32[384,1536]{0,1:T(8,128)} async-done(((f32[384,1536]{0,1:T(8,128)}), f32[384,1536]{0,1:T(8,128)}) %all-reduce.6.cloned.1.call-update) | async-done | bytes 2359312 | tf_op jit(solution)/shard_map/psum | solution.py:54
  494.4 1.9 broadcast_multiply_fusion
  496.2 2.0 copy.34
  (3 shorter events, 0.1 us)
Async XLA Ops:
  7.2 109.2 %all-gather.3.cloned.1.call-start = ((), (), s32[]{:S(2)}) async-start(), calls=%async_computation | async-start | bytes 13271040 | tf_op jit(solution)/shard_map/all_gather | solution.py:24
  12.5 241.0 %all-gather.5.cloned.1.call-start = ((), (), s32[]{:S(2)}) async-start(), calls=%async_computation.1 | async-start | bytes 7102464 | tf_op jit(solution)/shard_map/all_gather | solution.py:46
  116.3 1.3 slice-start
  129.3 0.8 copy-start.3
  129.3 2.8 copy-start
  130.2 0.8 copy-start.1
  132.1 194.7 %all-reduce.4.cloned.1.call-start = ((), (), s32[]{:S(2)}) async-start(), calls=%async_computation.2 | async-start | bytes 4718592 | tf_op jit(solution)/shard_map/psum | solution.py:54
  262.7 64.1 %copy-start.2 = (bf16[768,256]{1,0:T(8,128)(2,1)S(1)}, bf16[768,256]{1,0:T(8,128)(2,1)}, u32[]{:S(2)}) copy-start(bf16[768,256]{1,0:T(8,128)(2,1)} %copy-done.1) | copy-start | bytes 1179652
  262.8 231.6 %all-reduce.6.cloned.1.call-start = ((), (), s32[]{:S(2)}) async-start(), calls=%async_computation.3 | async-start | bytes 4718592 | tf_op jit(solution)/shard_map/psum | solution.py:54
Sparse Core Ops, SparseCore 0:
  12.7 103.6 all-gather.2
  132.2 121.3 all-gather.4
  262.9 63.8 all-reduce.3
  329.3 165.0 all-reduce.5

commit v3 on v2

--- a/solution.py
+++ b/solution.py
@@ -22,18 +22,18 @@
         [field, factor_t.reshape(factor_slabs, cells_three, cells_two, cells_one)], axis=0
     )
     joined_all = lax.all_gather(joined, "gx", axis=3, tiled=True)
-    piece = joined_all[:vars_all]
-    width = piece.shape[3]
+    width = joined_all.shape[3]
     factor_one_t = joined_all[vars_all:].reshape(factor_slabs * slab, width)[:rank_one]
 
+    local_rows = jnp.concatenate([field, jnp.zeros_like(joined[vars_all:])], axis=0)
     gram_block = lax.dot_general(
-        field.reshape(-1, cells_one),
-        piece.reshape(-1, width),
+        local_rows.reshape(-1, cells_one),
+        joined_all.reshape(-1, width),
         (((0,), (0,)), ((), ())),
         preferred_element_type=jnp.float32,
     )
 
-    own_vars = lax.dynamic_slice_in_dim(piece, lax.axis_index("gx") * own_rows, own_rows, axis=0)
+    own_vars = lax.dynamic_slice_in_dim(joined_all, lax.axis_index("gx") * own_rows, own_rows, axis=0)
     shrunk = lax.dot_general(
         own_vars.reshape(-1, width),
         factor_one_t,
@@ -43,14 +43,19 @@
 
     if rank_one == rank_two:
         extra = jnp.broadcast_to(mode_two_factor, (1, cells_three) + mode_two_factor.shape)
-        both_all = lax.all_gather(jnp.concatenate([shrunk, extra], axis=0), "gy", axis=2, tiled=True)
-        shrunk_all = both_all[:own_rows]
-        factor_two = both_all[own_rows, 0]
+        both = jnp.concatenate([shrunk, extra], axis=0)
     else:
-        shrunk_all = lax.all_gather(shrunk, "gy", axis=2, tiled=True)
+        both = shrunk
+    sent = jnp.broadcast_to(both[None], (count_gy,) + both.shape).reshape((-1,) + both.shape[1:])
+    got = lax.all_to_all(sent, "gy", 0, 0, tiled=True).reshape((count_gy,) + both.shape)
+    got = jnp.moveaxis(got, 0, 2).reshape(both.shape[:2] + (count_gy * cells_two, rank_one))
+    shrunk_all = got[:own_rows]
+    if rank_one == rank_two:
+        factor_two = got[own_rows, 0]
+    else:
         factor_two = lax.all_gather(mode_two_factor, "gy", axis=0, tiled=True)
 
-    gram_block, shrunk_all, factor_two = lax.optimization_barrier((gram_block, shrunk_all, factor_two))
+    gram_block, shrunk = lax.optimization_barrier((gram_block, shrunk))
     gram_sum = lax.psum(lax.psum(gram_block, "gz"), "gy")
     gram_one = gram_sum * (1.0 / (vars_all * total_three * total_two))
 

time: 505 us -> 490 us (0.970)
  matrix products: 26.3 us -> 15.6 us
  waiting for transfers between devices: 376 us -> 366 us
  starting transfers between devices: 0.34 us -> 9.7 us
    all_gather x1 -> x0, waiting for transfers between devices: 112 us -> none  [local(): lax.all_gather(jnp.concatenate([shrunk, extra], axis=0), 'gy', axis=2, ti...]
    psum x2, waiting for transfers between devices: 160 us -> 262 us  [local(): gram_sum = lax.psum(lax.psum(gram_block, 'gz'), 'gy')]
    slice x3, local copies, waits for them, and re-layouts: 16.9 us -> 5.11 us  [the longest x2 4.17 us: local(): shrunk_all = got[:own_rows]]
    all_to_all x0 -> x1, starting transfers between devices: none -> 9.58 us  [local(): lax.all_to_all(sent, 'gy', 0, 0, tiled=True)]
    dot_general x1, matrix products: 9.5 us -> 1.72 us  [local(): jnp.einsum('akjr,akqr->jq', shrunk, shrunk_all, preferred_element_type=jn...]
    transpose x0 -> x1, local copies, waits for them, and re-layouts: none -> 6.48 us  [local(): jnp.moveaxis(got, 0, 2)]
  transfers between devices with their start and end apart: 4 -> 4, of which waited for: 4 -> 3; matrix products, arithmetic and copies ran while one was open for 5% -> 2% of each run, Pallas kernels for 0% -> 0%
where the time goes in v3:
time: 490 us; the launch traced here: 489 us
  waiting for transfers between devices  366 us (75%)
  blocking collectives  52.7 us (11%)
  local copies, waits for them, and re-layouts  25.4 us (5%)
  matrix products  15.6 us (3%)
  between operations  13.9 us (3%)
  starting transfers between devices  9.7 us (2%)
  other arithmetic  5.81 us (1%)
    psum x2, waiting for transfers between devices, local(): gram_sum = lax.psum(lax.psum(gram_block, 'gz'), 'gy')  262 us
    all_gather x1, waiting for transfers between devices, local(): joined_all = lax.all_gather(joined, 'gx', axis=3, tiled=True)  104 us
    psum x1, blocking collectives, local(): lax.psum(gram_two_block, ('gx', 'gz'))  52.7 us
  transfers between devices with their start and end apart: 4, of which 3 were waited for; matrix products, arithmetic and copies ran while one was open for 2% of the time, Pallas kernels for 0%

profile of v3, /device:TPU:8, one launch (start us, length us, event | category | flops | bytes accessed | tf_op | source)
XLA Modules:
  0.0 488.7 jit_solution(3520355538818976272)
XLA Ops:
  7.2 0.0 all-gather.2.cloned.1.call-start
  7.2 1.1 copy.17
  8.3 0.1 copy.19
  8.4 2.2 copy.16
  10.7 1.9 pad_maximum_fusion
  12.5 0.0 all-gather.2.cloned.1.call-update
  12.5 103.8 %all-gather.2.cloned.1.call-done = bf16[70,2,24,1536]{3,0,2,1:T(8,128)(2,1)} async-done(((bf16[70,2,24,384]{3,0,2,1:T(8,128)(2,1)}), bf16[70,2,24,1536]{3,0,2,1:T(8,128)(2,1)}) %all-gather.2.cloned.1.call-update) | async-done | bytes 10321936 | tf_op jit(solution)/shard_map/all_gather | solution.py:24
  116.3 3.0 constant_dynamic-slice_fusion
  119.3 0.0 slice-start
  119.3 1.3 copy.20
  120.6 0.0 slice-done
  120.6 0.3 copy.21
  120.9 0.0 copy-start.1
  120.9 0.8 convolution_convert_fusion
  121.7 0.0 copy-done.1
  121.8 3.2 broadcast_in_dim.5
  125.0 9.6 %all-to-all-start = ((bf16[272,2,24,256]{3,2,1,0:T(8,128)(2,1)}), bf16[272,2,24,256]{3,2,1,0:T(8,128)(2,1)}, u32[]{:S(2)}, u32[]{:S(2)}) async-start(bf16[272,2,24,256]{3,2,1,0:T(8,128)(2,1)} %bitcast.36), calls=%async_computation | async-start | bytes 13369344 | tf_op jit(solution)/shard_map/all_to_all | solution.py:50
  134.6 0.0 all-reduce.5.cloned.1.call-start
  134.6 8.6 %convolution_bitcast_fusion = f32[384,1536]{1,0:T(8,128)} fusion(bf16[70,2,24,1536]{3,0,2,1:T(8,128)(2,1)} %all-gather.2.cloned.1.call-done, bf16[64,2,24,384]{3,0,2,1:T(8,128)(2,1)S(1)} %copy.16), kind=kOutput, calls=%fused_computation | convolution fusion | flops 3963617280 | bytes 15040512 | tf_op jit(solution)/shard_map/dot_general | solution.py:29
  143.2 0.0 all-reduce.5.cloned.1.call-update
  143.3 0.0 all-reduce.7.cloned.1.call-start
  143.3 69.1 %all-reduce.5.cloned.1.call-done = f32[384,1536]{1,0:T(8,128)} async-done(((f32[384,1536]{1,0:T(8,128)}), f32[384,1536]{1,0:T(8,128)}) %all-reduce.5.cloned.1.call-update) | async-done | bytes 2359312 | tf_op jit(solution)/shard_map/psum | solution.py:59
  212.4 0.0 all-reduce.7.cloned.1.call-update
  212.4 192.7 %all-reduce.7.cloned.1.call-done = f32[384,1536]{1,0:T(8,128)} async-done(((f32[384,1536]{1,0:T(8,128)}), f32[384,1536]{1,0:T(8,128)}) %all-reduce.7.cloned.1.call-update) | async-done | bytes 2359312 | tf_op jit(solution)/shard_map/psum | solution.py:59
  405.1 3.3 broadcast_multiply_fusion
  408.4 0.0 all-to-all-done
  408.4 3.4 slice.22
  411.8 6.5 %copy.23 = bf16[17,2,16,24,256]{4,3,2,1,0:T(8,128)(2,1)} copy(bf16[17,2,16,24,256]{4,3,1,0,2:T(8,128)(2,1)} %bitcast.9) | data formatting | bytes 13369344 | tf_op jit(solution)/shard_map/transpose | solution.py:51
  418.3 0.8 copy.22
  419.1 0.0 copy-start
  419.1 2.6 copy-done
  421.7 1.7 convolution_bitcast_fusion.1
  423.4 52.7 %psum.23 = f32[24,384]{1,0:T(8,128)S(1)} all-reduce(f32[24,384]{1,0:T(8,128)S(1)} %convolution_bitcast_fusion.1), channel_id=1, replica_groups=mesh['gx'=4,'gy'=16,'gz'=4] {'gx','gz'}, use_global_device_ids=true, to_apply=%region_2.3 | all-reduce | flops 9216 | bytes 73728 | tf_op jit(solution)/shard_map/psum | solution.py:65
  476.1 0.6 broadcast_multiply_fusion.1
  476.7 0.9 slice.23
  477.7 4.5 fusion.1
  (3 shorter events, 0.1 us)
Async XLA Ops:
  7.2 109.2 %all-gather.2.cloned.1.call-start = ((), (), s32[]{:S(2)}) async-start(), calls=%async_computation.1 | async-start | bytes 13271040 | tf_op jit(solution)/shard_map/all_gather | solution.py:24
  119.3 1.3 slice-start
  120.9 0.8 copy-start.1
  125.0 283.4 %all-to-all-start = ((bf16[272,2,24,256]{3,2,1,0:T(8,128)(2,1)}), bf16[272,2,24,256]{3,2,1,0:T(8,128)(2,1)}, u32[]{:S(2)}, u32[]{:S(2)}) async-start(bf16[272,2,24,256]{3,2,1,0:T(8,128)(2,1)} %bitcast.36), calls=%async_computation | async-start | bytes 13369344 | tf_op jit(solution)/shard_map/all_to_all | solution.py:50
  134.6 77.8 %all-reduce.5.cloned.1.call-start = ((), (), s32[]{:S(2)}) async-start(), calls=%async_computation.2 | async-start | bytes 4718592 | tf_op jit(solution)/shard_map/psum | solution.py:59
  143.3 261.9 %all-reduce.7.cloned.1.call-start = ((), (), s32[]{:S(2)}) async-start(), calls=%async_computation.3 | async-start | bytes 4718592 | tf_op jit(solution)/shard_map/psum | solution.py:59
  419.1 2.6 copy-start
Sparse Core Ops, SparseCore 0:
  12.7 103.6 all-gather.1
  143.4 68.9 all-reduce.4
  215.0 190.0 all-reduce.6

commit v4 on v1

--- a/solution.py
+++ b/solution.py
@@ -15,30 +15,50 @@
     rank_two = mode_two_factor.shape[1]
     own_ranks = rank_two // count_gy
 
-    factor_one = lax.all_gather(mode_one_factor, "gx", axis=0, tiled=True)
-    piece = lax.all_gather(field, "gx", axis=3, tiled=True)
+    product = jnp.dot(
+        field.reshape(-1, cells_one), mode_one_factor, preferred_element_type=jnp.float32
+    )
+    shrunk_sum = lax.psum_scatter(
+        product.reshape(vars_all, cells_three, cells_two, rank_one),
+        "gx",
+        scatter_dimension=0,
+        tiled=True,
+    )
+    field_later, shrunk_sum = lax.optimization_barrier((field, shrunk_sum))
+    shrunk = shrunk_sum.astype(jnp.bfloat16)
+
+    if rank_one == rank_two:
+        extra = jnp.broadcast_to(mode_two_factor, (1, cells_three) + mode_two_factor.shape)
+        both = jnp.concatenate([shrunk, extra], axis=0)
+    else:
+        both = shrunk
+    sent = jnp.broadcast_to(both[None], (count_gy,) + both.shape).reshape((-1,) + both.shape[1:])
+    got = lax.all_to_all(sent, "gy", 0, 0, tiled=True).reshape((count_gy,) + both.shape)
+
+    piece = lax.all_gather(field_later, "gx", axis=3, tiled=True)
     width = piece.shape[3]
     gram_block = lax.dot_general(
-        field.reshape(-1, cells_one),
+        field_later.reshape(-1, cells_one),
         piece.reshape(-1, width),
         (((0,), (0,)), ((), ())),
         preferred_element_type=jnp.float32,
     )
+    gram_block, got = lax.optimization_barrier((gram_block, got))
     gram_sum = lax.psum(lax.psum(gram_block, "gz"), "gy")
     gram_one = gram_sum * (1.0 / (vars_all * total_three * total_two))
 
-    own_vars = lax.dynamic_slice_in_dim(piece, lax.axis_index("gx") * own_rows, own_rows, axis=0)
-    shrunk = jnp.dot(
-        own_vars.reshape(-1, width), factor_one, preferred_element_type=jnp.float32
-    ).astype(jnp.bfloat16).reshape(own_rows, cells_three, cells_two, rank_one)
+    got = jnp.moveaxis(got, 0, 2).reshape(both.shape[:2] + (count_gy * cells_two, rank_one))
+    shrunk_all = got[:own_rows]
+    if rank_one == rank_two:
+        factor_two = got[own_rows, 0]
+    else:
+        factor_two = lax.all_gather(mode_two_factor, "gy", axis=0, tiled=True)
 
-    shrunk_all = lax.all_gather(shrunk, "gy", axis=2, tiled=True)
     gram_two_block = jnp.einsum(
         "akjr,akqr->jq", shrunk, shrunk_all, preferred_element_type=jnp.float32
     )
     gram_two = lax.psum(gram_two_block, ("gx", "gz")) * (1.0 / (vars_all * total_three * rank_one))
 
-    factor_two = lax.all_gather(mode_two_factor, "gy", axis=0, tiled=True)
     own_cols = lax.dynamic_slice_in_dim(factor_two, lax.axis_index("gy") * own_ranks, own_ranks, axis=1)
     core = jnp.einsum(
         "akjr,js->aksr", shrunk_all, own_cols, preferred_element_type=jnp.float32

time: 535 us -> 472 us (0.88)
  blocking collectives: 103 us -> 55.7 us
  waiting for transfers between devices: 392 us -> 351 us
  local copies, waits for them, and re-layouts: 1.83 us -> 17.4 us
  starting transfers between devices: 0.16 us -> 9.58 us
    all_gather x2 -> x1, waiting for transfers between devices: 209 us -> 149 us  [local(): piece = lax.all_gather(field_later, 'gx', axis=3, tiled=True)]
    all_gather x2 -> x0, blocking collectives: 50.8 us -> none  [the longest x1 42.2 us: local(): factor_two = lax.all_gather(mode_two_factor, 'gy', axis=0, tiled=True)]
    reduce_scatter x0 -> x1, waiting for transfers between devices: none -> 42.2 us  [local(): lax.psum_scatter(product.reshape(vars_all, cells_three, cells_two, rank_o...]
    psum x2, waiting for transfers between devices: 183 us -> 160 us  [local(): gram_sum = lax.psum(lax.psum(gram_block, 'gz'), 'gy')]
    all_to_all x0 -> x1, starting transfers between devices: none -> 9.41 us  [local(): lax.all_to_all(sent, 'gy', 0, 0, tiled=True)]
    transpose x0 -> x1, local copies, waits for them, and re-layouts: none -> 6.48 us  [local(): jnp.moveaxis(got, 0, 2)]
  transfers between devices with their start and end apart: 4 -> 5, of which waited for: 4 -> 4; matrix products, arithmetic and copies ran while one was open for 1% -> 7% of each run, Pallas kernels for 0% -> 0%
where the time goes in v4:
time: 472 us; the launch traced here: 471 us
  waiting for transfers between devices  351 us (74%)
  blocking collectives  55.7 us (12%)
  matrix products  18.4 us (4%)
  local copies, waits for them, and re-layouts  17.4 us (4%)
  between operations  13.8 us (3%)
  starting transfers between devices  9.58 us (2%)
  other arithmetic  5.12 us (1%)
    psum x2, waiting for transfers between devices, local(): gram_sum = lax.psum(lax.psum(gram_block, 'gz'), 'gy')  160 us
    all_gather x1, waiting for transfers between devices, local(): piece = lax.all_gather(field_later, 'gx', axis=3, tiled=True)  149 us
    psum x1, blocking collectives, local(): lax.psum(gram_two_block, ('gx', 'gz'))  55.7 us
    reduce_scatter x1, waiting for transfers between devices, local(): lax.psum_scatter(product.reshape(vars_all, cells_three, cells_two, rank_o...  42.2 us
  transfers between devices with their start and end apart: 5, of which 4 were waited for; matrix products, arithmetic and copies ran while one was open for 7% of the time, Pallas kernels for 0%

profile of v4, /device:TPU:8, one launch (start us, length us, event | category | flops | bytes accessed | tf_op | source)
XLA Modules:
  0.0 471.3 jit_solution(6557595521852024900)
XLA Ops:
  7.2 0.0 copy-start
  7.2 0.0 reduce-scatter.2.cloned.1.call-start
  7.2 0.9 copy-done
  8.1 4.3 fusion.1
  12.4 0.0 copy-start.3
  12.4 0.0 reduce-scatter.2.cloned.1.call-update
  12.4 0.0 all-gather.2.cloned.1.call-start
  12.5 42.2 %reduce-scatter.2.cloned.1.call-done = f32[16,2,24,256]{3,2,1,0:T(8,128)} async-done(((f32[64,2,24,256]{3,2,1,0:T(8,128)}), f32[16,2,24,256]{3,2,1,0:T(8,128)}) %reduce-scatter.2.cloned.1.call-update) | async-done | bytes 786448 | tf_op jit(solution)/shard_map/reduce_scatter | solution.py:21
  54.7 0.0 all-gather.2.cloned.1.call-update
  54.7 1.2 convert_element_type.9
  55.9 0.0 copy-done.3
  56.0 3.2 broadcast_in_dim.10
  59.2 0.0 copy-start.2
  59.2 9.4 %all-to-all-start = ((bf16[272,2,24,256]{3,2,1,0:T(8,128)(2,1)}), bf16[272,2,24,256]{3,2,1,0:T(8,128)(2,1)}, u32[]{:S(2)}, u32[]{:S(2)}) async-start(bf16[272,2,24,256]{3,2,1,0:T(8,128)(2,1)} %bitcast.36), calls=%async_computation.1 | async-start | bytes 13369344 | tf_op jit(solution)/shard_map/all_to_all | solution.py:36
  68.6 0.0 all-reduce.3.cloned.1.call-start
  68.6 148.5 %all-gather.2.cloned.1.call-done = bf16[64,2,24,1536]{3,2,1,0:T(8,128)(2,1)} async-done(((bf16[64,2,24,384]{3,2,1,0:T(8,128)(2,1)}), bf16[64,2,24,1536]{3,2,1,0:T(8,128)(2,1)}) %all-gather.2.cloned.1.call-update) | async-done | bytes 9437200 | tf_op jit(solution)/shard_map/all_gather | solution.py:38
  217.2 0.0 copy-done.2
  217.2 7.8 %convolution_bitcast_fusion = f32[384,1536]{1,0:T(8,128)} fusion(bf16[64,2,24,384]{3,2,1,0:T(8,128)(2,1)S(1)} %copy-done.2, bf16[64,2,24,1536]{3,2,1,0:T(8,128)(2,1)} %all-gather.2.cloned.1.call-done), kind=kOutput, calls=%fused_computation | convolution fusion | flops 3623878656 | bytes 14155776 | tf_op jit(solution)/shard_map/dot_general | solution.py:40
  225.0 0.0 all-to-all-done
  225.0 0.0 all-reduce.3.cloned.1.call-update
  225.0 0.0 all-reduce.5.cloned.1.call-start
  225.1 68.8 %all-reduce.3.cloned.1.call-done = f32[384,1536]{1,0:T(8,128)} async-done(((f32[384,1536]{1,0:T(8,128)}), f32[384,1536]{1,0:T(8,128)}) %all-reduce.3.cloned.1.call-update) | async-done | bytes 2359312 | tf_op jit(solution)/shard_map/psum | solution.py:47
  293.9 0.0 all-reduce.5.cloned.1.call-update
  293.9 3.4 slice.12
  297.3 6.5 %copy.13 = bf16[17,2,16,24,256]{4,3,2,1,0:T(8,128)(2,1)} copy(bf16[17,2,16,24,256]{4,3,1,0,2:T(8,128)(2,1)} %bitcast.6) | data formatting | bytes 13369344 | tf_op jit(solution)/shard_map/transpose | solution.py:50
  303.8 0.8 copy.12
  304.6 0.0 copy-start.1
  304.6 1.2 slice.13
  305.8 1.5 copy-done.1
  307.2 1.7 convolution_bitcast_fusion.1
  309.0 55.7 %psum.23 = f32[24,384]{1,0:T(8,128)S(1)} all-reduce(f32[24,384]{1,0:T(8,128)S(1)} %convolution_bitcast_fusion.1), channel_id=1, replica_groups=mesh['gx'=4,'gy'=16,'gz'=4] {'gx','gz'}, use_global_device_ids=true, to_apply=%region_3.0 | all-reduce | flops 9216 | bytes 73728 | tf_op jit(solution)/shard_map/psum | solution.py:60
  364.7 0.6 broadcast_multiply_fusion.1
  365.3 4.5 fusion
  369.8 91.6 %all-reduce.5.cloned.1.call-done = f32[384,1536]{1,0:T(8,128)} async-done(((f32[384,1536]{1,0:T(8,128)}), f32[384,1536]{1,0:T(8,128)}) %all-reduce.5.cloned.1.call-update) | async-done | bytes 2359312 | tf_op jit(solution)/shard_map/psum | solution.py:47
  461.5 3.3 broadcast_multiply_fusion
  (2 shorter events, 0.0 us)
Async XLA Ops:
  7.2 0.9 copy-start
  7.2 47.5 %reduce-scatter.2.cloned.1.call-start = ((), (), s32[]{:S(2)}) async-start(), calls=%async_computation.2 | async-start | bytes 3932160 | tf_op jit(solution)/shard_map/reduce_scatter | solution.py:21
  12.4 43.5 %copy-start.3 = (bf16[24,256]{1,0:T(8,128)(2,1)S(1)}, bf16[24,256]{1,0:T(8,128)(2,1)}, u32[]{:S(2)}) copy-start(bf16[24,256]{1,0:T(8,128)(2,1)} %param.5) | copy-start | bytes 36868
  12.4 204.8 %all-gather.2.cloned.1.call-start = ((), (), s32[]{:S(2)}) async-start(), calls=%async_computation.3 | async-start | bytes 11796480 | tf_op jit(solution)/shard_map/all_gather | solution.py:38
  59.2 158.0 %copy-start.2 = (bf16[64,2,24,384]{3,2,1,0:T(8,128)(2,1)S(1)}, bf16[64,2,24,384]{3,2,1,0:T(8,128)(2,1)}, u32[]{:S(2)}) copy-start(bf16[64,2,24,384]{3,2,1,0:T(8,128)(2,1)} %param.3) | copy-start | bytes 7077892
  59.2 165.8 %all-to-all-start = ((bf16[272,2,24,256]{3,2,1,0:T(8,128)(2,1)}), bf16[272,2,24,256]{3,2,1,0:T(8,128)(2,1)}, u32[]{:S(2)}, u32[]{:S(2)}) async-start(bf16[272,2,24,256]{3,2,1,0:T(8,128)(2,1)} %bitcast.36), calls=%async_computation.1 | async-start | bytes 13369344 | tf_op jit(solution)/shard_map/all_to_all | solution.py:36
  68.6 225.3 %all-reduce.3.cloned.1.call-start = ((), (), s32[]{:S(2)}) async-start(), calls=%async_computation.4 | async-start | bytes 4718592 | tf_op jit(solution)/shard_map/psum | solution.py:47
  225.0 236.4 %all-reduce.5.cloned.1.call-start = ((), (), s32[]{:S(2)}) async-start(), calls=%async_computation.5 | async-start | bytes 4718592 | tf_op jit(solution)/shard_map/psum | solution.py:47
  304.6 2.6 copy-start.1
Sparse Core Ops, SparseCore 0:
  12.5 42.1 reduce-scatter.1
  56.5 160.6 all-gather.1
  225.1 68.7 all-reduce.2
  296.4 165.0 all-reduce.4

commit v5 on v4

--- a/solution.py
+++ b/solution.py
@@ -44,9 +44,6 @@
         preferred_element_type=jnp.float32,
     )
     gram_block, got = lax.optimization_barrier((gram_block, got))
-    gram_sum = lax.psum(lax.psum(gram_block, "gz"), "gy")
-    gram_one = gram_sum * (1.0 / (vars_all * total_three * total_two))
-
     got = jnp.moveaxis(got, 0, 2).reshape(both.shape[:2] + (count_gy * cells_two, rank_one))
     shrunk_all = got[:own_rows]
     if rank_one == rank_two:
@@ -57,7 +54,17 @@
     gram_two_block = jnp.einsum(
         "akjr,akqr->jq", shrunk, shrunk_all, preferred_element_type=jnp.float32
     )
-    gram_two = lax.psum(gram_two_block, ("gx", "gz")) * (1.0 / (vars_all * total_three * rank_one))
+    two_size = gram_two_block.size
+    extra_rows = -(-two_size // width)
+    extra_rows = -(-extra_rows // 8) * 8
+    two_rows = jnp.pad(gram_two_block.reshape(-1), (0, extra_rows * width - two_size))
+    stacked = jnp.concatenate([gram_block, two_rows.reshape(extra_rows, width)], axis=0)
+    stacked = lax.psum(stacked, "gz")
+    own_gram = stacked.shape[0] - extra_rows
+    gram_sum = lax.psum(stacked[:own_gram], "gy")
+    gram_one = gram_sum * (1.0 / (vars_all * total_three * total_two))
+    two_sum = stacked[own_gram:].reshape(-1)[:two_size].reshape(gram_two_block.shape)
+    gram_two = lax.psum(two_sum, "gx") * (1.0 / (vars_all * total_three * rank_one))
 
     own_cols = lax.dynamic_slice_in_dim(factor_two, lax.axis_index("gy") * own_ranks, own_ranks, axis=1)
     core = jnp.einsum(

time: 472 us -> 484 us (1.025)
  waiting for transfers between devices: 351 us -> 406 us
  blocking collectives: 55.7 us -> 12.2 us
    psum x2, waiting for transfers between devices: 160 us -> 216 us  [the longest x1 146 us: local(): gram_sum = lax.psum(stacked[:own_gram], 'gy')]
    psum x1, blocking collectives: 55.7 us -> 12.2 us  [local(): lax.psum(two_sum, 'gx') * (1.0 / (vars_all * total_three * rank_one))]
  transfers between devices with their start and end apart: 5 -> 5, of which waited for: 4 -> 4; matrix products, arithmetic and copies ran while one was open for 7% -> 4% of each run, Pallas kernels for 0% -> 0%
where the time goes in v5:
time: 484 us; the launch traced here: 483 us
  waiting for transfers between devices  406 us (84%)
  local copies, waits for them, and re-layouts  20 us (4%)
  matrix products  15.5 us (3%)
  between operations  13.9 us (3%)
  blocking collectives  12.2 us (3%)
  starting transfers between devices  9.58 us (2%)
  other arithmetic  5.57 us (1%)
    all_gather x1, waiting for transfers between devices, local(): piece = lax.all_gather(field_later, 'gx', axis=3, tiled=True)  149 us
    psum x1, waiting for transfers between devices, local(): gram_sum = lax.psum(stacked[:own_gram], 'gy')  146 us
    psum x1, waiting for transfers between devices, local(): stacked = lax.psum(stacked, 'gz')  69.7 us
    reduce_scatter x1, waiting for transfers between devices, local(): lax.psum_scatter(product.reshape(vars_all, cells_three, cells_two, rank_o...  42.2 us
    psum x1, blocking collectives, local(): lax.psum(two_sum, 'gx') * (1.0 / (vars_all * total_three * rank_one))  12.2 us
  transfers between devices with their start and end apart: 5, of which 4 were waited for; matrix products, arithmetic and copies ran while one was open for 4% of the time, Pallas kernels for 0%

profile of v5, /device:TPU:8, one launch (start us, length us, event | category | flops | bytes accessed | tf_op | source)
XLA Modules:
  0.0 483.2 jit_solution(10370210913449993104)
XLA Ops:
  7.2 0.0 copy-start
  7.2 0.0 reduce-scatter.2.cloned.1.call-start
  7.2 0.9 copy-done
  8.1 4.3 fusion.1
  12.4 0.0 reduce-scatter.2.cloned.1.call-update
  12.4 0.0 copy-start.5
  12.4 0.0 all-gather.2.cloned.1.call-start
  12.5 42.2 %reduce-scatter.2.cloned.1.call-done = f32[16,2,24,256]{3,2,1,0:T(8,128)} async-done(((f32[64,2,24,256]{3,2,1,0:T(8,128)}), f32[16,2,24,256]{3,2,1,0:T(8,128)}) %reduce-scatter.2.cloned.1.call-update) | async-done | bytes 786448 | tf_op jit(solution)/shard_map/reduce_scatter | solution.py:21
  54.7 0.0 copy-start.4
  54.7 0.0 all-gather.2.cloned.1.call-update
  54.7 1.1 copy-done.4
  55.9 0.0 copy-done.5
  55.9 3.2 broadcast_in_dim.10
  59.1 0.0 copy-start.2
  59.1 9.4 %all-to-all-start = ((bf16[272,2,24,256]{3,2,1,0:T(8,128)(2,1)}), bf16[272,2,24,256]{3,2,1,0:T(8,128)(2,1)}, u32[]{:S(2)}, u32[]{:S(2)}) async-start(bf16[272,2,24,256]{3,2,1,0:T(8,128)(2,1)} %bitcast.38), calls=%async_computation.1 | async-start | bytes 13369344 | tf_op jit(solution)/shard_map/all_to_all | solution.py:36
  68.5 0.0 all-reduce.4.cloned.1.call-start
  68.6 148.6 %all-gather.2.cloned.1.call-done = bf16[64,2,24,1536]{3,2,1,0:T(8,128)(2,1)} async-done(((bf16[64,2,24,384]{3,2,1,0:T(8,128)(2,1)}), bf16[64,2,24,1536]{3,2,1,0:T(8,128)(2,1)}) %all-gather.2.cloned.1.call-update) | async-done | bytes 9437200 | tf_op jit(solution)/shard_map/all_gather | solution.py:38
  217.1 0.0 copy-done.2
  217.2 7.8 %convolution_bitcast_fusion = f32[384,1536]{1,0:T(8,128)} fusion(bf16[64,2,24,384]{3,2,1,0:T(8,128)(2,1)S(1)} %copy-done.2, bf16[64,2,24,1536]{3,2,1,0:T(8,128)(2,1)} %all-gather.2.cloned.1.call-done), kind=kOutput, calls=%fused_computation | convolution fusion | flops 3623878656 | bytes 14155776 | tf_op jit(solution)/shard_map/dot_general | solution.py:40
  225.0 0.0 all-to-all-done
  225.0 3.4 slice.23
  228.4 0.8 copy.12
  229.1 0.0 copy-start.1
  229.2 2.6 copy-done.1
  231.8 0.0 copy-start.3
  231.8 1.7 convolution_bitcast_fusion.1
  233.6 0.0 copy-done.3
  233.6 1.6 pad_maximum_fusion
  235.2 0.0 all-reduce.4.cloned.1.call-update
  235.2 0.0 all-reduce.6.cloned.1.call-start
  235.2 69.7 %all-reduce.4.cloned.1.call-done = f32[392,1536]{1,0:T(8,128)} async-done(((f32[392,1536]{1,0:T(8,128)}), f32[392,1536]{1,0:T(8,128)}) %all-reduce.4.cloned.1.call-update) | async-done | bytes 2408464 | tf_op jit(solution)/shard_map/psum | solution.py:62
  304.9 3.2 slice.24
  308.2 0.0 slice-start
  308.2 0.0 all-reduce.6.cloned.1.call-update
  308.2 0.0 slice-start.1
  308.2 3.9 copy.13
  312.1 0.0 slice-done
  312.1 0.8 slice-done.1
  312.9 0.0 slice-start.2
  312.9 1.7 fusion
  314.6 0.0 slice-done.2
  314.7 12.2 %psum.23 = f32[24,384]{1,0:T(8,128)S(1)} all-reduce(f32[24,384]{1,0:T(8,128)S(1)} %reshape.40), channel_id=1, replica_groups=mesh['gx'=4,'gy'=16,'gz'=4] {'gx'}, use_global_device_ids=true, to_apply=%region_3.4 | all-reduce | flops 9216 | bytes 73728 | tf_op jit(solution)/shard_map/psum | solution.py:67
  326.8 0.6 broadcast_multiply_fusion.1
  327.4 146.0 %all-reduce.6.cloned.1.call-done = f32[384,1536]{1,0:T(8,128)} async-done(((f32[384,1536]{1,0:T(8,128)}), f32[384,1536]{1,0:T(8,128)}) %all-reduce.6.cloned.1.call-update) | async-done | bytes 2359312 | tf_op jit(solution)/shard_map/psum | solution.py:64
  473.4 3.3 broadcast_multiply_fusion
  (9 shorter events, 0.1 us)
Async XLA Ops:
  7.2 0.9 copy-start
  7.2 47.5 %reduce-scatter.2.cloned.1.call-start = ((), (), s32[]{:S(2)}) async-start(), calls=%async_computation.2 | async-start | bytes 3932160 | tf_op jit(solution)/shard_map/reduce_scatter | solution.py:21
  12.4 43.5 %copy-start.5 = (bf16[24,256]{1,0:T(8,128)(2,1)S(1)}, bf16[24,256]{1,0:T(8,128)(2,1)}, u32[]{:S(2)}) copy-start(bf16[24,256]{1,0:T(8,128)(2,1)} %param.5) | copy-start | bytes 36868
  12.4 204.7 %all-gather.2.cloned.1.call-start = ((), (), s32[]{:S(2)}) async-start(), calls=%async_computation.3 | async-start | bytes 11796480 | tf_op jit(solution)/shard_map/all_gather | solution.py:38
  54.7 1.1 copy-start.4
  59.1 158.0 %copy-start.2 = (bf16[64,2,24,384]{3,2,1,0:T(8,128)(2,1)S(1)}, bf16[64,2,24,384]{3,2,1,0:T(8,128)(2,1)}, u32[]{:S(2)}) copy-start(bf16[64,2,24,384]{3,2,1,0:T(8,128)(2,1)} %param.3) | copy-start | bytes 7077892
  59.1 165.8 %all-to-all-start = ((bf16[272,2,24,256]{3,2,1,0:T(8,128)(2,1)}), bf16[272,2,24,256]{3,2,1,0:T(8,128)(2,1)}, u32[]{:S(2)}, u32[]{:S(2)}) async-start(bf16[272,2,24,256]{3,2,1,0:T(8,128)(2,1)} %bitcast.38), calls=%async_computation.1 | async-start | bytes 13369344 | tf_op jit(solution)/shard_map/all_to_all | solution.py:36
  68.5 236.4 %all-reduce.4.cloned.1.call-start = ((), (), s32[]{:S(2)}) async-start(), calls=%async_computation.4 | async-start | bytes 4816896 | tf_op jit(solution)/shard_map/psum | solution.py:62
  229.1 2.6 copy-start.1
  231.8 1.8 copy-start.3
  235.2 238.2 %all-reduce.6.cloned.1.call-start = ((), (), s32[]{:S(2)}) async-start(), calls=%async_computation.5 | async-start | bytes 4718592 | tf_op jit(solution)/shard_map/psum | solution.py:64
  308.2 3.9 slice-start
  308.2 4.7 slice-start.1
  312.9 1.7 slice-start.2
Sparse Core Ops, SparseCore 0:
  12.5 42.1 reduce-scatter.1
  56.5 160.5 all-gather.1
  235.3 69.5 all-reduce.3
  308.3 165.0 all-reduce.5

commit v6 on v4

--- a/solution.py
+++ b/solution.py
@@ -44,7 +44,12 @@
         preferred_element_type=jnp.float32,
     )
     gram_block, got = lax.optimization_barrier((gram_block, got))
-    gram_sum = lax.psum(lax.psum(gram_block, "gz"), "gy")
+    slice_rows = gram_block.shape[0] // count_gy
+    parts = lax.all_to_all(gram_block, "gy", 0, 0, tiled=True)
+    own_slice = jnp.sum(parts.reshape(count_gy, slice_rows, width), axis=0)
+    own_slice = lax.psum(own_slice, "gz")
+    copies = jnp.broadcast_to(own_slice[None], (count_gy,) + own_slice.shape).reshape(-1, width)
+    gram_sum = lax.all_to_all(copies, "gy", 0, 0, tiled=True)
     gram_one = gram_sum * (1.0 / (vars_all * total_three * total_two))
 
     got = jnp.moveaxis(got, 0, 2).reshape(both.shape[:2] + (count_gy * cells_two, rank_one))

time: 472 us -> 435 us (0.922)
  waiting for transfers between devices: 351 us -> 233 us
  blocking collectives: 55.7 us -> 122 us
  starting transfers between devices: 9.58 us -> 19.1 us
    psum x2 -> x1, waiting for transfers between devices: 160 us -> 42.1 us  [local(): own_slice = lax.psum(own_slice, 'gz')]
    all_to_all x0 -> x1, blocking collectives: none -> 67 us  [local(): parts = lax.all_to_all(gram_block, 'gy', 0, 0, tiled=True)]
    all_to_all x0 -> x1, starting transfers between devices: none -> 9.53 us  [local(): gram_sum = lax.all_to_all(copies, 'gy', 0, 0, tiled=True)]
  transfers between devices with their start and end apart: 5 -> 5, of which waited for: 4 -> 3; matrix products, arithmetic and copies ran while one was open for 7% -> 7% of each run, Pallas kernels for 0% -> 0%
where the time goes in v6:
time: 435 us; the launch traced here: 430 us
  waiting for transfers between devices  233 us (54%)
  blocking collectives  122 us (28%)
  local copies, waits for them, and re-layouts  19.9 us (5%)
  starting transfers between devices  19.1 us (4%)
  matrix products  18.3 us (4%)
  between operations  13.8 us (3%)
    all_gather x1, waiting for transfers between devices, local(): piece = lax.all_gather(field_later, 'gx', axis=3, tiled=True)  149 us
    all_to_all x1, blocking collectives, local(): parts = lax.all_to_all(gram_block, 'gy', 0, 0, tiled=True)  67 us
    psum x1, blocking collectives, local(): lax.psum(gram_two_block, ('gx', 'gz'))  55 us
    reduce_scatter x1, waiting for transfers between devices, local(): lax.psum_scatter(product.reshape(vars_all, cells_three, cells_two, rank_o...  42.2 us
    psum x1, waiting for transfers between devices, local(): own_slice = lax.psum(own_slice, 'gz')  42.1 us
    all_to_all x1, starting transfers between devices, local(): gram_sum = lax.all_to_all(copies, 'gy', 0, 0, tiled=True)  9.53 us
    all_to_all x1, starting transfers between devices, local(): lax.all_to_all(sent, 'gy', 0, 0, tiled=True)  9.41 us
  transfers between devices with their start and end apart: 5, of which 3 were waited for; matrix products, arithmetic and copies ran while one was open for 7% of the time, Pallas kernels for 0%

profile of v6, /device:TPU:8, one launch (start us, length us, event | category | flops | bytes accessed | tf_op | source)
XLA Modules:
  0.0 430.4 jit_solution(2106228878218715670)
XLA Ops:
  7.2 0.0 copy-start
  7.2 0.0 reduce-scatter.2.cloned.1.call-start
  7.2 0.9 copy-done
  8.1 4.3 %fusion.1 = f32[64,2,24,256]{3,2,1,0:T(8,128)} fusion(bf16[64,2,24,384]{3,2,1,0:T(8,128)(2,1)} %param.3, bf16[384,256]{1,0:T(8,128)(2,1)S(1)} %copy-done), kind=kOutput, calls=%fused_computation.6 | convolution fusion | flops 603979776 | bytes 5701632 | tf_op jit(solution)/shard_map/dot_general | solution.py:18
  12.4 0.0 copy-start.3
  12.4 0.0 reduce-scatter.2.cloned.1.call-update
  12.4 0.0 all-gather.2.cloned.1.call-start
  12.5 42.2 %reduce-scatter.2.cloned.1.call-done = f32[16,2,24,256]{3,2,1,0:T(8,128)} async-done(((f32[64,2,24,256]{3,2,1,0:T(8,128)}), f32[16,2,24,256]{3,2,1,0:T(8,128)}) %reduce-scatter.2.cloned.1.call-update) | async-done | bytes 786448 | tf_op jit(solution)/shard_map/reduce_scatter | solution.py:21
  54.7 0.0 all-gather.2.cloned.1.call-update
  54.7 1.2 convert_element_type.9
  55.9 0.0 copy-done.3
  56.0 3.2 broadcast_in_dim.7
  59.2 0.0 copy-start.2
  59.2 9.4 %all-to-all-start = ((bf16[272,2,24,256]{3,2,1,0:T(8,128)(2,1)}), bf16[272,2,24,256]{3,2,1,0:T(8,128)(2,1)}, u32[]{:S(2)}, u32[]{:S(2)}) async-start(bf16[272,2,24,256]{3,2,1,0:T(8,128)(2,1)} %bitcast.38), calls=%async_computation.1 | async-start | bytes 13369344 | tf_op jit(solution)/shard_map/all_to_all | solution.py:36
  68.6 0.0 all-reduce.2.cloned.1.call-start
  68.6 148.5 %all-gather.2.cloned.1.call-done = bf16[64,2,24,1536]{3,2,1,0:T(8,128)(2,1)} async-done(((bf16[64,2,24,384]{3,2,1,0:T(8,128)(2,1)}), bf16[64,2,24,1536]{3,2,1,0:T(8,128)(2,1)}) %all-gather.2.cloned.1.call-update) | async-done | bytes 9437200 | tf_op jit(solution)/shard_map/all_gather | solution.py:38
  217.2 0.0 copy-done.2
  217.2 7.8 %convolution_bitcast_fusion = f32[384,1536]{1,0:T(8,128)} fusion(bf16[64,2,24,384]{3,2,1,0:T(8,128)(2,1)S(1)} %copy-done.2, bf16[64,2,24,1536]{3,2,1,0:T(8,128)(2,1)} %all-gather.2.cloned.1.call-done), kind=kOutput, calls=%fused_computation | convolution fusion | flops 3623878656 | bytes 14155776 | tf_op jit(solution)/shard_map/dot_general | solution.py:40
  225.0 0.0 all-to-all-done
  225.0 67.0 %all_to_all.20 = f32[16,24,1536]{2,1,0:T(8,128)S(1)} all-to-all(f32[16,24,1536]{2,1,0:T(8,128)} %bitcast.40), channel_id=1, replica_groups=mesh['gx'=4,'gy'=16,'gz'=4] {'gy'}, dimensions={0} | all-to-all | bytes 4718592 | tf_op jit(solution)/shard_map/all_to_all | solution.py:48
  292.0 0.8 reduce_sum.9
  292.8 0.0 all-reduce.2.cloned.1.call-update
  292.8 42.1 %all-reduce.2.cloned.1.call-done = f32[24,1536]{1,0:T(8,128)} async-done(((f32[24,1536]{1,0:T(8,128)}), f32[24,1536]{1,0:T(8,128)}) %all-reduce.2.cloned.1.call-update) | async-done | bytes 147472 | tf_op jit(solution)/shard_map/psum | solution.py:50
  334.9 2.6 broadcast_in_dim.8
  337.5 9.5 %all-to-all-start.2 = ((f32[16,24,1536]{2,1,0:T(8,128)}), f32[16,24,1536]{2,1,0:T(8,128)S(1)}, u32[]{:S(2)}, u32[]{:S(2)}) async-start(f32[16,24,1536]{2,1,0:T(8,128)} %broadcast_in_dim.8), calls=%async_computation.3 | async-start | bytes 4718592 | tf_op jit(solution)/shard_map/all_to_all | solution.py:52
  347.1 3.4 slice.12
  350.5 6.5 %copy.13 = bf16[17,2,16,24,256]{4,3,2,1,0:T(8,128)(2,1)} copy(bf16[17,2,16,24,256]{4,3,1,0,2:T(8,128)(2,1)} %bitcast.8) | data formatting | bytes 13369344 | tf_op jit(solution)/shard_map/transpose | solution.py:55
  357.0 0.8 copy.12
  357.7 0.0 copy-start.1
  357.7 1.2 slice.13
  358.9 1.4 copy-done.1
  360.4 1.7 convolution_bitcast_fusion.1
  362.1 55.0 %psum.15 = f32[24,384]{1,0:T(8,128)S(1)} all-reduce(f32[24,384]{1,0:T(8,128)S(1)} %convolution_bitcast_fusion.1), channel_id=1, replica_groups=mesh['gx'=4,'gy'=16,'gz'=4] {'gx','gz'}, use_global_device_ids=true, to_apply=%region_3.0 | all-reduce | flops 9216 | bytes 73728 | tf_op jit(solution)/shard_map/psum | solution.py:65
  417.1 0.6 broadcast_multiply_fusion.1
  417.7 4.5 %fusion = bf16[16,2,16,256]{3,2,1,0:T(8,128)(2,1)} fusion(bf16[16,2,384,256]{3,2,1,0:T(8,128)(2,1)} %bitcast.37, bf16[1,1,384,256]{3,2,1,0:T(8,128)(2,1)S(1)} %slice.13, s32[]{:T(128)S(6)} %select_n.3), kind=kOutput, calls=%fused_computation.3 | convolution fusion | flops 100794368 | bytes 6651908 | tf_op jit(solution)/shard_map/akjr,js->aksr/dot_general | solution.py:68
  422.2 0.0 all-to-all-done.2
  422.2 1.6 broadcast_multiply_fusion
  (2 shorter events, 0.0 us)
Async XLA Ops:
  7.2 0.9 copy-start
  7.2 47.5 %reduce-scatter.2.cloned.1.call-start = ((), (), s32[]{:S(2)}) async-start(), calls=%async_computation.4 | async-start | bytes 3932160 | tf_op jit(solution)/shard_map/reduce_scatter | solution.py:21
  12.4 43.5 %copy-start.3 = (bf16[24,256]{1,0:T(8,128)(2,1)S(1)}, bf16[24,256]{1,0:T(8,128)(2,1)}, u32[]{:S(2)}) copy-start(bf16[24,256]{1,0:T(8,128)(2,1)} %param.5) | copy-start | bytes 36868
  12.4 204.8 %all-gather.2.cloned.1.call-start = ((), (), s32[]{:S(2)}) async-start(), calls=%async_computation.5 | async-start | bytes 11796480 | tf_op jit(solution)/shard_map/all_gather | solution.py:38
  59.2 158.0 %copy-start.2 = (bf16[64,2,24,384]{3,2,1,0:T(8,128)(2,1)S(1)}, bf16[64,2,24,384]{3,2,1,0:T(8,128)(2,1)}, u32[]{:S(2)}) copy-start(bf16[64,2,24,384]{3,2,1,0:T(8,128)(2,1)} %param.3) | copy-start | bytes 7077892
  59.2 165.8 %all-to-all-start = ((bf16[272,2,24,256]{3,2,1,0:T(8,128)(2,1)}), bf16[272,2,24,256]{3,2,1,0:T(8,128)(2,1)}, u32[]{:S(2)}, u32[]{:S(2)}) async-start(bf16[272,2,24,256]{3,2,1,0:T(8,128)(2,1)} %bitcast.38), calls=%async_computation.1 | async-start | bytes 13369344 | tf_op jit(solution)/shard_map/all_to_all | solution.py:36
  68.6 266.3 %all-reduce.2.cloned.1.call-start = ((), (), s32[]{:S(2)}) async-start(), calls=%async_computation.6 | async-start | bytes 294912 | tf_op jit(solution)/shard_map/psum | solution.py:50
  337.5 84.7 %all-to-all-start.2 = ((f32[16,24,1536]{2,1,0:T(8,128)}), f32[16,24,1536]{2,1,0:T(8,128)S(1)}, u32[]{:S(2)}, u32[]{:S(2)}) async-start(f32[16,24,1536]{2,1,0:T(8,128)} %broadcast_in_dim.8), calls=%async_computation.3 | async-start | bytes 4718592 | tf_op jit(solution)/shard_map/all_to_all | solution.py:52
  357.7 2.6 copy-start.1
Sparse Core Ops, SparseCore 0:
  12.6 42.1 reduce-scatter.1
  56.5 160.6 all-gather.1
  293.0 41.9 all-reduce.1

commit v7 on v5

--- a/solution.py
+++ b/solution.py
@@ -50,20 +50,23 @@
         factor_two = got[own_rows, 0]
     else:
         factor_two = lax.all_gather(mode_two_factor, "gy", axis=0, tiled=True)
-
     gram_two_block = jnp.einsum(
         "akjr,akqr->jq", shrunk, shrunk_all, preferred_element_type=jnp.float32
     )
+
+    slice_rows = gram_block.shape[0] // count_gy
+    parts = lax.all_to_all(gram_block, "gy", 0, 0, tiled=True)
+    own_slice = jnp.sum(parts.reshape(count_gy, slice_rows, width), axis=0)
     two_size = gram_two_block.size
     extra_rows = -(-two_size // width)
     extra_rows = -(-extra_rows // 8) * 8
     two_rows = jnp.pad(gram_two_block.reshape(-1), (0, extra_rows * width - two_size))
-    stacked = jnp.concatenate([gram_block, two_rows.reshape(extra_rows, width)], axis=0)
-    stacked = lax.psum(stacked, "gz")
-    own_gram = stacked.shape[0] - extra_rows
-    gram_sum = lax.psum(stacked[:own_gram], "gy")
+    stacked = lax.psum(jnp.concatenate([own_slice, two_rows.reshape(extra_rows, width)], axis=0), "gz")
+    own_slice = stacked[:slice_rows]
+    copies = jnp.broadcast_to(own_slice[None], (count_gy,) + own_slice.shape).reshape(-1, width)
+    gram_sum = lax.all_to_all(copies, "gy", 0, 0, tiled=True)
     gram_one = gram_sum * (1.0 / (vars_all * total_three * total_two))
-    two_sum = stacked[own_gram:].reshape(-1)[:two_size].reshape(gram_two_block.shape)
+    two_sum = stacked[slice_rows:].reshape(-1)[:two_size].reshape(gram_two_block.shape)
     gram_two = lax.psum(two_sum, "gx") * (1.0 / (vars_all * total_three * rank_one))
 
     own_cols = lax.dynamic_slice_in_dim(factor_two, lax.axis_index("gy") * own_ranks, own_ranks, axis=1)

time: 484 us -> 417 us (0.86)
  waiting for transfers between devices: 406 us -> 322 us
  starting transfers between devices: 9.58 us -> 29 us
    psum x2 -> x1, waiting for transfers between devices: 216 us -> 46.7 us  [local(): lax.psum(jnp.concatenate([own_slice, two_rows.reshape(extra_rows, width)]...]
    all_to_all x0 -> x2, waiting for transfers between devices: none -> 84.8 us  [the longest x1 47.3 us: local(): parts = lax.all_to_all(gram_block, 'gy', 0, 0, tiled=True)]
    all_to_all x0 -> x2, starting transfers between devices: none -> 19.5 us  [the longest x1 9.76 us: local(): parts = lax.all_to_all(gram_block, 'gy', 0, 0, tiled=True)]
  transfers between devices with their start and end apart: 5 -> 6, of which waited for: 4 -> 5; matrix products, arithmetic and copies ran while one was open for 4% -> 6% of each run, Pallas kernels for 0% -> 0%
where the time goes in v7:
time: 417 us; the launch traced here: 416 us
  waiting for transfers between devices  322 us (77%)
  starting transfers between devices  29 us (7%)
  local copies, waits for them, and re-layouts  17.6 us (4%)
  matrix products  15.5 us (4%)
  between operations  13.9 us (3%)
  blocking collectives  11.6 us (3%)
  other arithmetic  5.94 us (1%)
    all_gather x1, waiting for transfers between devices, local(): piece = lax.all_gather(field_later, 'gx', axis=3, tiled=True)  149 us
    all_to_all x1, waiting for transfers between devices, local(): parts = lax.all_to_all(gram_block, 'gy', 0, 0, tiled=True)  47.3 us
    psum x1, waiting for transfers between devices, local(): lax.psum(jnp.concatenate([own_slice, two_rows.reshape(extra_rows, width)]...  46.7 us
    reduce_scatter x1, waiting for transfers between devices, local(): lax.psum_scatter(product.reshape(vars_all, cells_three, cells_two, rank_o...  42.2 us
    all_to_all x1, waiting for transfers between devices, local(): gram_sum = lax.all_to_all(copies, 'gy', 0, 0, tiled=True)  37.5 us
    psum x1, blocking collectives, local(): lax.psum(two_sum, 'gx') * (1.0 / (vars_all * total_three * rank_one))  11.6 us
    all_to_all x1, starting transfers between devices, local(): parts = lax.all_to_all(gram_block, 'gy', 0, 0, tiled=True)  9.76 us
    all_to_all x1, starting transfers between devices, local(): gram_sum = lax.all_to_all(copies, 'gy', 0, 0, tiled=True)  9.71 us
  transfers between devices with their start and end apart: 6, of which 5 were waited for; matrix products, arithmetic and copies ran while one was open for 6% of the time, Pallas kernels for 0%

profile of v7, /device:TPU:8, one launch (start us, length us, event | category | flops | bytes accessed | tf_op | source)
XLA Modules:
  0.0 416.0 jit_solution(177366309837097245)
XLA Ops:
  7.2 0.0 copy-start
  7.2 0.0 reduce-scatter.2.cloned.1.call-start
  7.2 0.9 copy-done
  8.1 4.3 %fusion.1 = f32[64,2,24,256]{3,2,1,0:T(8,128)} fusion(bf16[64,2,24,384]{3,2,1,0:T(8,128)(2,1)} %param.3, bf16[384,256]{1,0:T(8,128)(2,1)S(1)} %copy-done), kind=kOutput, calls=%fused_computation.7 | convolution fusion | flops 603979776 | bytes 5701632 | tf_op jit(solution)/shard_map/dot_general | solution.py:18
  12.4 0.0 copy-start.3
  12.4 0.0 reduce-scatter.2.cloned.1.call-update
  12.4 0.0 all-gather.2.cloned.1.call-start
  12.5 42.2 %reduce-scatter.2.cloned.1.call-done = f32[16,2,24,256]{3,2,1,0:T(8,128)} async-done(((f32[64,2,24,256]{3,2,1,0:T(8,128)}), f32[16,2,24,256]{3,2,1,0:T(8,128)}) %reduce-scatter.2.cloned.1.call-update) | async-done | bytes 786448 | tf_op jit(solution)/shard_map/reduce_scatter | solution.py:21
  54.7 0.0 all-gather.2.cloned.1.call-update
  54.7 1.2 convert_element_type.11
  55.9 0.0 copy-done.3
  56.0 3.2 broadcast_in_dim.7
  59.1 0.0 copy-start.2
  59.2 9.4 %all-to-all-start = ((bf16[272,2,24,256]{3,2,1,0:T(8,128)(2,1)}), bf16[272,2,24,256]{3,2,1,0:T(8,128)(2,1)}, u32[]{:S(2)}, u32[]{:S(2)}) async-start(bf16[272,2,24,256]{3,2,1,0:T(8,128)(2,1)} %bitcast.40), calls=%async_computation.1 | async-start | bytes 13369344 | tf_op jit(solution)/shard_map/all_to_all | solution.py:36
  68.6 148.6 %all-gather.2.cloned.1.call-done = bf16[64,2,24,1536]{3,2,1,0:T(8,128)(2,1)} async-done(((bf16[64,2,24,384]{3,2,1,0:T(8,128)(2,1)}), bf16[64,2,24,1536]{3,2,1,0:T(8,128)(2,1)}) %all-gather.2.cloned.1.call-update) | async-done | bytes 9437200 | tf_op jit(solution)/shard_map/all_gather | solution.py:38
  217.2 0.0 copy-done.2
  217.2 7.8 %convolution_bitcast_fusion = f32[384,1536]{1,0:T(8,128)} fusion(bf16[64,2,24,384]{3,2,1,0:T(8,128)(2,1)S(1)} %copy-done.2, bf16[64,2,24,1536]{3,2,1,0:T(8,128)(2,1)} %all-gather.2.cloned.1.call-done), kind=kOutput, calls=%fused_computation | convolution fusion | flops 3623878656 | bytes 14155776 | tf_op jit(solution)/shard_map/dot_general | solution.py:40
  225.0 0.0 all-to-all-done
  225.0 9.8 %all-to-all-start.1 = ((f32[16,24,1536]{2,1,0:T(8,128)}), f32[16,24,1536]{2,1,0:T(8,128)S(1)}, u32[]{:S(2)}, u32[]{:S(2)}) async-start(f32[16,24,1536]{2,1,0:T(8,128)} %bitcast.42), calls=%async_computation.2 | async-start | bytes 4718592 | tf_op jit(solution)/shard_map/all_to_all | solution.py:58
  234.7 0.0 all-reduce.3.cloned.1.call-start
  234.8 3.4 slice.23
  238.2 0.8 copy.12
  239.0 0.0 copy-start.1
  239.0 2.6 copy-done.1
  241.6 1.7 convolution_bitcast_fusion.1
  243.4 47.3 %all-to-all-done.1 = f32[16,24,1536]{2,1,0:T(8,128)S(1)} async-done(((f32[16,24,1536]{2,1,0:T(8,128)}), f32[16,24,1536]{2,1,0:T(8,128)S(1)}, u32[]{:S(2)}, u32[]{:S(2)}) %all-to-all-start.1) | async-done | bytes 2359328 | tf_op jit(solution)/shard_map/all_to_all | solution.py:58
  290.8 0.1 reduce_sum.9
  290.9 0.7 pad_maximum_fusion.1
  291.6 0.0 all-reduce.3.cloned.1.call-update
  291.6 46.7 %all-reduce.3.cloned.1.call-done = f32[32,1536]{1,0:T(8,128)} async-done(((f32[32,1536]{1,0:T(8,128)}), f32[32,1536]{1,0:T(8,128)}) %all-reduce.3.cloned.1.call-update) | async-done | bytes 196624 | tf_op jit(solution)/shard_map/psum | solution.py:64
  338.3 0.9 slice.24
  339.2 1.7 broadcast_in_dim.8
  340.9 0.0 slice-start
  340.9 9.7 %all-to-all-start.2 = ((f32[16,24,1536]{2,1,0:T(8,128)}), f32[16,24,1536]{2,1,0:T(8,128)}, u32[]{:S(2)}, u32[]{:S(2)}) async-start(f32[16,24,1536]{2,1,0:T(8,128)} %broadcast_in_dim.8), calls=%async_computation.3 | async-start | bytes 4718592 | tf_op jit(solution)/shard_map/all_to_all | solution.py:67
  350.6 0.0 slice-start.1
  350.6 3.9 copy.13
  354.5 0.0 slice-done
  354.5 0.2 slice-done.1
  354.7 0.0 slice-start.2
  354.7 1.7 fusion
  356.4 0.0 slice-done.2
  356.5 11.6 %psum.15 = f32[24,384]{1,0:T(8,128)S(1)} all-reduce(f32[24,384]{1,0:T(8,128)S(1)} %reshape.51), channel_id=1, replica_groups=mesh['gx'=4,'gy'=16,'gz'=4] {'gx'}, use_global_device_ids=true, to_apply=%region_3.4 | all-reduce | flops 9216 | bytes 73728 | tf_op jit(solution)/shard_map/psum | solution.py:70
  368.1 0.6 broadcast_multiply_fusion.1
  368.7 37.5 %all-to-all-done.2 = f32[16,24,1536]{2,1,0:T(8,128)} async-done(((f32[16,24,1536]{2,1,0:T(8,128)}), f32[16,24,1536]{2,1,0:T(8,128)}, u32[]{:S(2)}, u32[]{:S(2)}) %all-to-all-start.2) | async-done | bytes 2359328 | tf_op jit(solution)/shard_map/all_to_all | solution.py:67
  406.2 3.3 broadcast_multiply_fusion
  (8 shorter events, 0.1 us)
Async XLA Ops:
  7.2 0.9 copy-start
  7.2 47.5 %reduce-scatter.2.cloned.1.call-start = ((), (), s32[]{:S(2)}) async-start(), calls=%async_computation.4 | async-start | bytes 3932160 | tf_op jit(solution)/shard_map/reduce_scatter | solution.py:21
  12.4 43.5 %copy-start.3 = (bf16[24,256]{1,0:T(8,128)(2,1)S(1)}, bf16[24,256]{1,0:T(8,128)(2,1)}, u32[]{:S(2)}) copy-start(bf16[24,256]{1,0:T(8,128)(2,1)} %param.5) | copy-start | bytes 36868
  12.4 204.8 %all-gather.2.cloned.1.call-start = ((), (), s32[]{:S(2)}) async-start(), calls=%async_computation.5 | async-start | bytes 11796480 | tf_op jit(solution)/shard_map/all_gather | solution.py:38
  59.1 158.0 %copy-start.2 = (bf16[64,2,24,384]{3,2,1,0:T(8,128)(2,1)S(1)}, bf16[64,2,24,384]{3,2,1,0:T(8,128)(2,1)}, u32[]{:S(2)}) copy-start(bf16[64,2,24,384]{3,2,1,0:T(8,128)(2,1)} %param.3) | copy-start | bytes 7077892
  59.2 165.8 %all-to-all-start = ((bf16[272,2,24,256]{3,2,1,0:T(8,128)(2,1)}), bf16[272,2,24,256]{3,2,1,0:T(8,128)(2,1)}, u32[]{:S(2)}, u32[]{:S(2)}) async-start(bf16[272,2,24,256]{3,2,1,0:T(8,128)(2,1)} %bitcast.40), calls=%async_computation.1 | async-start | bytes 13369344 | tf_op jit(solution)/shard_map/all_to_all | solution.py:36
  225.0 65.8 %all-to-all-start.1 = ((f32[16,24,1536]{2,1,0:T(8,128)}), f32[16,24,1536]{2,1,0:T(8,128)S(1)}, u32[]{:S(2)}, u32[]{:S(2)}) async-start(f32[16,24,1536]{2,1,0:T(8,128)} %bitcast.42), calls=%async_computation.2 | async-start | bytes 4718592 | tf_op jit(solution)/shard_map/all_to_all | solution.py:58
  234.7 103.5 %all-reduce.3.cloned.1.call-start = ((), (), s32[]{:S(2)}) async-start(), calls=%async_computation.6 | async-start | bytes 393216 | tf_op jit(solution)/shard_map/psum | solution.py:64
  239.0 2.7 copy-start.1
  340.9 13.6 %slice-start = ((s8[6291456]{0:T(1024)(128)(4,1)}), s8[2097152]{0:T(1024)(128)(4,1)S(1)}, s32[]{:S(2)}) async-start(s8[6291456]{0:T(1024)(128)(4,1)} %bitcast.37), calls=%async_computation.7 | async-start | bytes 4194304
  340.9 65.3 %all-to-all-start.2 = ((f32[16,24,1536]{2,1,0:T(8,128)}), f32[16,24,1536]{2,1,0:T(8,128)}, u32[]{:S(2)}, u32[]{:S(2)}) async-start(f32[16,24,1536]{2,1,0:T(8,128)} %broadcast_in_dim.8), calls=%async_computation.3 | async-start | bytes 4718592 | tf_op jit(solution)/shard_map/all_to_all | solution.py:67
  350.6 4.1 slice-start.1
  354.7 1.7 slice-start.2
Sparse Core Ops, SparseCore 0:
  12.5 42.1 reduce-scatter.1
  56.5 160.6 all-gather.1
  291.7 46.4 all-reduce.2

commit v8 on v6

--- a/solution.py
+++ b/solution.py
@@ -32,8 +32,7 @@
         both = jnp.concatenate([shrunk, extra], axis=0)
     else:
         both = shrunk
-    sent = jnp.broadcast_to(both[None], (count_gy,) + both.shape).reshape((-1,) + both.shape[1:])
-    got = lax.all_to_all(sent, "gy", 0, 0, tiled=True).reshape((count_gy,) + both.shape)
+    sent_early = jnp.broadcast_to(both[None], (count_gy,) + both.shape).reshape((-1,) + both.shape[1:])
 
     piece = lax.all_gather(field_later, "gx", axis=3, tiled=True)
     width = piece.shape[3]
@@ -43,11 +42,14 @@
         (((0,), (0,)), ((), ())),
         preferred_element_type=jnp.float32,
     )
+    sent, gram_block = lax.optimization_barrier((sent_early, gram_block))
+    got = lax.all_to_all(sent, "gy", 0, 0, tiled=True).reshape((count_gy,) + both.shape)
+    gram_block = lax.psum(gram_block, "gz")
     gram_block, got = lax.optimization_barrier((gram_block, got))
+
     slice_rows = gram_block.shape[0] // count_gy
     parts = lax.all_to_all(gram_block, "gy", 0, 0, tiled=True)
     own_slice = jnp.sum(parts.reshape(count_gy, slice_rows, width), axis=0)
-    own_slice = lax.psum(own_slice, "gz")
     copies = jnp.broadcast_to(own_slice[None], (count_gy,) + own_slice.shape).reshape(-1, width)
     gram_sum = lax.all_to_all(copies, "gy", 0, 0, tiled=True)
     gram_one = gram_sum * (1.0 / (vars_all * total_three * total_two))
@@ -58,11 +60,10 @@
         factor_two = got[own_rows, 0]
     else:
         factor_two = lax.all_gather(mode_two_factor, "gy", axis=0, tiled=True)
-
     gram_two_block = jnp.einsum(
         "akjr,akqr->jq", shrunk, shrunk_all, preferred_element_type=jnp.float32
     )
-    gram_two = lax.psum(gram_two_block, ("gx", "gz")) * (1.0 / (vars_all * total_three * rank_one))
+    gram_two = lax.psum(lax.psum(gram_two_block, "gx"), "gz") * (1.0 / (vars_all * total_three * rank_one))
 
     own_cols = lax.dynamic_slice_in_dim(factor_two, lax.axis_index("gy") * own_ranks, own_ranks, axis=1)
     core = jnp.einsum(

time: 435 us -> 461 us (1.060)
  waiting for transfers between devices: 233 us -> 297 us
  blocking collectives: 122 us -> 94 us
  starting transfers between devices: 19.1 us -> 14.3 us
    all_to_all x1, waiting for transfers between devices: 0.01 us -> 78.5 us  [local(): lax.all_to_all(sent, 'gy', 0, 0, tiled=True)]
    all_gather x1, waiting for transfers between devices: 149 us -> 92.7 us  [local(): piece = lax.all_gather(field_later, 'gx', axis=3, tiled=True)]
    psum x1, waiting for transfers between devices: 42.1 us -> 72 us  [local(): gram_block = lax.psum(gram_block, 'gz')]
    psum x1 -> x2, blocking collectives: 55 us -> 26.4 us  [the longest x1 15.1 us: local(): lax.psum(lax.psum(gram_two_block, 'gx'), 'gz')]
    all_to_all x1, waiting for transfers between devices: 0.01 us -> 10.5 us  [local(): gram_sum = lax.all_to_all(copies, 'gy', 0, 0, tiled=True)]
    all_to_all x1, starting transfers between devices: 9.53 us -> 4.77 us  [local(): gram_sum = lax.all_to_all(copies, 'gy', 0, 0, tiled=True)]
  transfers between devices with their start and end apart: 5 -> 5, of which waited for: 3 -> 5; matrix products, arithmetic and copies ran while one was open for 7% -> 4% of each run, Pallas kernels for 0% -> 0%
where the time goes in v8:
time: 461 us; the launch traced here: 460 us
  waiting for transfers between devices  297 us (64%)
  blocking collectives  94 us (20%)
  local copies, waits for them, and re-layouts  19.2 us (4%)
  matrix products  18.3 us (4%)
  starting transfers between devices  14.3 us (3%)
  between operations  13.9 us (3%)
    all_gather x1, waiting for transfers between devices, local(): piece = lax.all_gather(field_later, 'gx', axis=3, tiled=True)  92.7 us
    all_to_all x1, waiting for transfers between devices, local(): lax.all_to_all(sent, 'gy', 0, 0, tiled=True)  78.5 us
    psum x1, waiting for transfers between devices, local(): gram_block = lax.psum(gram_block, 'gz')  72 us
    all_to_all x1, blocking collectives, local(): parts = lax.all_to_all(gram_block, 'gy', 0, 0, tiled=True)  67.6 us
    reduce_scatter x1, waiting for transfers between devices, local(): lax.psum_scatter(product.reshape(vars_all, cells_three, cells_two, rank_o...  42.2 us
    psum x1, blocking collectives, local(): lax.psum(lax.psum(gram_two_block, 'gx'), 'gz')  15.1 us
    psum x1, blocking collectives, local(): lax.psum(gram_two_block, 'gx')  11.3 us
    all_to_all x1, waiting for transfers between devices, local(): gram_sum = lax.all_to_all(copies, 'gy', 0, 0, tiled=True)  10.5 us
  transfers between devices with their start and end apart: 5, of which 5 were waited for; matrix products, arithmetic and copies ran while one was open for 4% of the time, Pallas kernels for 0%

profile of v8, /device:TPU:8, one launch (start us, length us, event | category | flops | bytes accessed | tf_op | source)
XLA Modules:
  0.0 460.0 jit_solution(8518680385397478713)
XLA Ops:
  7.2 0.0 copy-start
  7.2 0.0 reduce-scatter.2.cloned.1.call-start
  7.2 0.9 copy-done
  8.1 4.3 fusion.1
  12.4 0.0 copy-start.3
  12.4 0.0 copy-start.2
  12.4 0.0 reduce-scatter.2.cloned.1.call-update
  12.4 0.0 all-gather.2.cloned.1.call-start
  12.5 42.2 %reduce-scatter.2.cloned.1.call-done = f32[16,2,24,256]{3,2,1,0:T(8,128)} async-done(((f32[64,2,24,256]{3,2,1,0:T(8,128)}), f32[16,2,24,256]{3,2,1,0:T(8,128)}) %reduce-scatter.2.cloned.1.call-update) | async-done | bytes 786448 | tf_op jit(solution)/shard_map/reduce_scatter | solution.py:21
  54.7 0.0 all-gather.2.cloned.1.call-update
  54.7 1.2 convert_element_type.9
  55.9 0.0 copy-done.3
  56.0 92.7 %all-gather.2.cloned.1.call-done = bf16[64,2,24,1536]{3,2,1,0:T(8,128)(2,1)} async-done(((bf16[64,2,24,384]{3,2,1,0:T(8,128)(2,1)}), bf16[64,2,24,1536]{3,2,1,0:T(8,128)(2,1)}) %all-gather.2.cloned.1.call-update) | async-done | bytes 9437200 | tf_op jit(solution)/shard_map/all_gather | solution.py:37
  148.7 0.0 copy-done.2
  148.7 7.8 %convolution_bitcast_fusion = f32[384,1536]{1,0:T(8,128)} fusion(bf16[64,2,24,384]{3,2,1,0:T(8,128)(2,1)S(1)} %copy-done.2, bf16[64,2,24,1536]{3,2,1,0:T(8,128)(2,1)} %all-gather.2.cloned.1.call-done), kind=kOutput, calls=%fused_computation | convolution fusion | flops 3623878656 | bytes 14155776 | tf_op jit(solution)/shard_map/dot_general | solution.py:39
  156.5 3.2 broadcast_in_dim.7
  159.7 9.4 %all-to-all-start = ((bf16[272,2,24,256]{3,2,1,0:T(8,128)(2,1)}), bf16[272,2,24,256]{3,2,1,0:T(8,128)(2,1)}, u32[]{:S(2)}, u32[]{:S(2)}) async-start(bf16[272,2,24,256]{3,2,1,0:T(8,128)(2,1)} %bitcast.38), calls=%async_computation.1 | async-start | bytes 13369344 | tf_op jit(solution)/shard_map/all_to_all | solution.py:46
  169.1 0.0 all-reduce.2.cloned.1.call-start
  169.2 0.7 all-reduce.2.cloned.1.call-update
  169.9 72.0 %all-reduce.2.cloned.1.call-done = f32[384,1536]{1,0:T(8,128)} async-done(((f32[384,1536]{1,0:T(8,128)}), f32[384,1536]{1,0:T(8,128)}) %all-reduce.2.cloned.1.call-update) | async-done | bytes 2359312 | tf_op jit(solution)/shard_map/psum | solution.py:47
  241.9 78.5 %all-to-all-done = bf16[272,2,24,256]{3,2,1,0:T(8,128)(2,1)} async-done(((bf16[272,2,24,256]{3,2,1,0:T(8,128)(2,1)}), bf16[272,2,24,256]{3,2,1,0:T(8,128)(2,1)}, u32[]{:S(2)}, u32[]{:S(2)}) %all-to-all-start) | async-done | bytes 6684704 | tf_op jit(solution)/shard_map/all_to_all | solution.py:46
  320.4 67.6 %all_to_all.20 = f32[16,24,1536]{2,1,0:T(8,128)S(1)} all-to-all(f32[16,24,1536]{2,1,0:T(8,128)} %bitcast.40), channel_id=1, replica_groups=mesh['gx'=4,'gy'=16,'gz'=4] {'gy'}, dimensions={0} | all-to-all | bytes 4718592 | tf_op jit(solution)/shard_map/all_to_all | solution.py:51
  388.0 0.1 reduce_sum.9
  388.2 1.7 broadcast_in_dim.8
  389.9 4.8 %all-to-all-start.2 = ((f32[16,24,1536]{2,1,0:T(8,128)}), f32[16,24,1536]{2,1,0:T(8,128)S(1)}, u32[]{:S(2)}, u32[]{:S(2)}) async-start(f32[16,24,1536]{2,1,0:T(8,128)} %broadcast_in_dim.8), calls=%async_computation.3 | async-start | bytes 4718592 | tf_op jit(solution)/shard_map/all_to_all | solution.py:54
  394.6 3.4 slice.12
  398.0 6.5 %copy.13 = bf16[17,2,16,24,256]{4,3,2,1,0:T(8,128)(2,1)} copy(bf16[17,2,16,24,256]{4,3,1,0,2:T(8,128)(2,1)} %bitcast.8) | data formatting | bytes 13369344 | tf_op jit(solution)/shard_map/transpose | solution.py:57
  404.6 0.8 copy.12
  405.4 0.0 copy-start.1
  405.4 1.2 slice.13
  406.5 1.5 copy-done.1
  408.0 1.7 convolution_bitcast_fusion.1
  409.7 11.3 %psum.22 = f32[24,384]{1,0:T(8,128)S(1)} all-reduce(f32[24,384]{1,0:T(8,128)S(1)} %convolution_bitcast_fusion.1), channel_id=1, replica_groups=mesh['gx'=4,'gy'=16,'gz'=4] {'gx'}, use_global_device_ids=true, to_apply=%region_3.0 | all-reduce | flops 9216 | bytes 73728 | tf_op jit(solution)/shard_map/psum | solution.py:66
  421.0 15.1 %psum.23 = f32[24,384]{1,0:T(8,128)S(1)} all-reduce(f32[24,384]{1,0:T(8,128)S(1)} %psum.22), channel_id=1, replica_groups=mesh['gx'=4,'gy'=16,'gz'=4] {'gz'}, use_global_device_ids=true, to_apply=%region_4.0 | all-reduce | flops 9216 | bytes 73728 | tf_op jit(solution)/shard_map/psum | solution.py:66
  436.2 0.6 broadcast_multiply_fusion.1
  436.8 4.5 fusion
  441.3 10.5 %all-to-all-done.2 = f32[16,24,1536]{2,1,0:T(8,128)S(1)} async-done(((f32[16,24,1536]{2,1,0:T(8,128)}), f32[16,24,1536]{2,1,0:T(8,128)S(1)}, u32[]{:S(2)}, u32[]{:S(2)}) %all-to-all-start.2) | async-done | bytes 2359328 | tf_op jit(solution)/shard_map/all_to_all | solution.py:54
  451.8 1.6 broadcast_multiply_fusion
  (2 shorter events, 0.0 us)
Async XLA Ops:
  7.2 0.9 copy-start
  7.2 47.5 %reduce-scatter.2.cloned.1.call-start = ((), (), s32[]{:S(2)}) async-start(), calls=%async_computation.4 | async-start | bytes 3932160 | tf_op jit(solution)/shard_map/reduce_scatter | solution.py:21
  12.4 43.5 %copy-start.3 = (bf16[24,256]{1,0:T(8,128)(2,1)S(1)}, bf16[24,256]{1,0:T(8,128)(2,1)}, u32[]{:S(2)}) copy-start(bf16[24,256]{1,0:T(8,128)(2,1)} %param.5) | copy-start | bytes 36868
  12.4 136.3 %copy-start.2 = (bf16[64,2,24,384]{3,2,1,0:T(8,128)(2,1)S(1)}, bf16[64,2,24,384]{3,2,1,0:T(8,128)(2,1)}, u32[]{:S(2)}) copy-start(bf16[64,2,24,384]{3,2,1,0:T(8,128)(2,1)} %param.3) | copy-start | bytes 7077892
  12.4 136.2 %all-gather.2.cloned.1.call-start = ((), (), s32[]{:S(2)}) async-start(), calls=%async_computation.5 | async-start | bytes 11796480 | tf_op jit(solution)/shard_map/all_gather | solution.py:37
  159.7 160.7 %all-to-all-start = ((bf16[272,2,24,256]{3,2,1,0:T(8,128)(2,1)}), bf16[272,2,24,256]{3,2,1,0:T(8,128)(2,1)}, u32[]{:S(2)}, u32[]{:S(2)}) async-start(bf16[272,2,24,256]{3,2,1,0:T(8,128)(2,1)} %bitcast.38), calls=%async_computation.1 | async-start | bytes 13369344 | tf_op jit(solution)/shard_map/all_to_all | solution.py:46
  169.1 72.8 %all-reduce.2.cloned.1.call-start = ((), (), s32[]{:S(2)}) async-start(), calls=%async_computation.6 | async-start | bytes 4718592 | tf_op jit(solution)/shard_map/psum | solution.py:47
  389.9 62.0 %all-to-all-start.2 = ((f32[16,24,1536]{2,1,0:T(8,128)}), f32[16,24,1536]{2,1,0:T(8,128)S(1)}, u32[]{:S(2)}, u32[]{:S(2)}) async-start(f32[16,24,1536]{2,1,0:T(8,128)} %broadcast_in_dim.8), calls=%async_computation.3 | async-start | bytes 4718592 | tf_op jit(solution)/shard_map/all_to_all | solution.py:54
  405.4 2.7 copy-start.1
Sparse Core Ops, SparseCore 0:
  12.6 42.1 reduce-scatter.1
  56.5 92.0 all-gather.1
  172.9 68.9 all-reduce.1

commit v9 on v7

--- a/solution.py
+++ b/solution.py
@@ -61,7 +61,14 @@
     extra_rows = -(-two_size // width)
     extra_rows = -(-extra_rows // 8) * 8
     two_rows = jnp.pad(gram_two_block.reshape(-1), (0, extra_rows * width - two_size))
-    stacked = lax.psum(jnp.concatenate([own_slice, two_rows.reshape(extra_rows, width)], axis=0), "gz")
+    stacked = jnp.concatenate([own_slice, two_rows.reshape(extra_rows, width)], axis=0)
+    count_gz = lax.axis_size("gz")
+    chunk = -(-stacked.shape[0] // (8 * count_gz)) * 8
+    stacked = jnp.pad(stacked, ((0, chunk * count_gz - stacked.shape[0]), (0, 0)))
+    pieces = lax.all_to_all(stacked, "gz", 0, 0, tiled=True)
+    own_chunk = jnp.sum(pieces.reshape(count_gz, chunk, width), axis=0)
+    chunk_copies = jnp.broadcast_to(own_chunk[None], (count_gz,) + own_chunk.shape).reshape(-1, width)
+    stacked = lax.all_to_all(chunk_copies, "gz", 0, 0, tiled=True)
     own_slice = stacked[:slice_rows]
     copies = jnp.broadcast_to(own_slice[None], (count_gy,) + own_slice.shape).reshape(-1, width)
     gram_sum = lax.all_to_all(copies, "gy", 0, 0, tiled=True)

time: 417 us -> 385 us (0.923)
  waiting for transfers between devices: 322 us -> 273 us
  blocking collectives: 11.6 us -> 30.1 us
    psum x1 -> x0, waiting for transfers between devices: 46.7 us -> none  [local(): lax.psum(jnp.concatenate([own_slice, two_rows.reshape(extra_rows, width)]...]
    all_to_all x0 -> x2, blocking collectives: none -> 18.2 us  [the longest x1 9.5 us: local(): pieces = lax.all_to_all(stacked, 'gz', 0, 0, tiled=True)]
  transfers between devices with their start and end apart: 6 -> 5, of which waited for: 5 -> 4; matrix products, arithmetic and copies ran while one was open for 6% -> 6% of each run, Pallas kernels for 0% -> 0%
where the time goes in v9:
time: 385 us; the launch traced here: 384 us
  waiting for transfers between devices  273 us (71%)
  blocking collectives  30.1 us (8%)
  starting transfers between devices  28.5 us (7%)
  local copies, waits for them, and re-layouts  16.8 us (4%)
  matrix products  15.6 us (4%)
  between operations  14.2 us (4%)
  other arithmetic  5.28 us (1%)
    all_gather x1, waiting for transfers between devices, local(): piece = lax.all_gather(field_later, 'gx', axis=3, tiled=True)  149 us
    all_to_all x1, waiting for transfers between devices, local(): parts = lax.all_to_all(gram_block, 'gy', 0, 0, tiled=True)  47.4 us
    reduce_scatter x1, waiting for transfers between devices, local(): lax.psum_scatter(product.reshape(vars_all, cells_three, cells_two, rank_o...  42.2 us
    all_to_all x1, waiting for transfers between devices, local(): gram_sum = lax.all_to_all(copies, 'gy', 0, 0, tiled=True)  35 us
    psum x1, blocking collectives, local(): lax.psum(two_sum, 'gx') * (1.0 / (vars_all * total_three * rank_one))  11.9 us
    all_to_all x1, starting transfers between devices, local(): parts = lax.all_to_all(gram_block, 'gy', 0, 0, tiled=True)  9.75 us
    all_to_all x1, blocking collectives, local(): pieces = lax.all_to_all(stacked, 'gz', 0, 0, tiled=True)  9.5 us
    all_to_all x1, starting transfers between devices, local(): lax.all_to_all(sent, 'gy', 0, 0, tiled=True)  9.41 us
  transfers between devices with their start and end apart: 5, of which 4 were waited for; matrix products, arithmetic and copies ran while one was open for 6% of the time, Pallas kernels for 0%

profile of v9, /device:TPU:8, one launch (start us, length us, event | category | flops | bytes accessed | tf_op | source)
XLA Modules:
  0.0 383.6 jit_solution(6135498418313631793)
XLA Ops:
  7.2 0.0 copy-start
  7.2 0.0 reduce-scatter.2.cloned.1.call-start
  7.2 0.9 copy-done
  8.1 4.3 %fusion.1 = f32[64,2,24,256]{3,2,1,0:T(8,128)} fusion(bf16[64,2,24,384]{3,2,1,0:T(8,128)(2,1)} %param.3, bf16[384,256]{1,0:T(8,128)(2,1)S(1)} %copy-done), kind=kOutput, calls=%fused_computation.7 | convolution fusion | flops 603979776 | bytes 5701632 | tf_op jit(solution)/shard_map/dot_general | solution.py:18
  12.4 0.0 copy-start.3
  12.4 0.0 reduce-scatter.2.cloned.1.call-update
  12.4 0.0 all-gather.2.cloned.1.call-start
  12.5 42.2 %reduce-scatter.2.cloned.1.call-done = f32[16,2,24,256]{3,2,1,0:T(8,128)} async-done(((f32[64,2,24,256]{3,2,1,0:T(8,128)}), f32[16,2,24,256]{3,2,1,0:T(8,128)}) %reduce-scatter.2.cloned.1.call-update) | async-done | bytes 786448 | tf_op jit(solution)/shard_map/reduce_scatter | solution.py:21
  54.7 0.0 all-gather.2.cloned.1.call-update
  54.7 1.2 convert_element_type.11
  55.9 0.0 copy-done.3
  56.0 3.2 broadcast_in_dim.11
  59.1 0.0 copy-start.2
  59.1 9.4 %all-to-all-start = ((bf16[272,2,24,256]{3,2,1,0:T(8,128)(2,1)}), bf16[272,2,24,256]{3,2,1,0:T(8,128)(2,1)}, u32[]{:S(2)}, u32[]{:S(2)}) async-start(bf16[272,2,24,256]{3,2,1,0:T(8,128)(2,1)} %bitcast.44), calls=%async_computation.1 | async-start | bytes 13369344 | tf_op jit(solution)/shard_map/all_to_all | solution.py:36
  68.6 148.6 %all-gather.2.cloned.1.call-done = bf16[64,2,24,1536]{3,2,1,0:T(8,128)(2,1)} async-done(((bf16[64,2,24,384]{3,2,1,0:T(8,128)(2,1)}), bf16[64,2,24,1536]{3,2,1,0:T(8,128)(2,1)}) %all-gather.2.cloned.1.call-update) | async-done | bytes 9437200 | tf_op jit(solution)/shard_map/all_gather | solution.py:38
  217.2 0.0 copy-done.2
  217.2 7.8 %convolution_bitcast_fusion = f32[384,1536]{1,0:T(8,128)} fusion(bf16[64,2,24,384]{3,2,1,0:T(8,128)(2,1)S(1)} %copy-done.2, bf16[64,2,24,1536]{3,2,1,0:T(8,128)(2,1)} %all-gather.2.cloned.1.call-done), kind=kOutput, calls=%fused_computation | convolution fusion | flops 3623878656 | bytes 14155776 | tf_op jit(solution)/shard_map/dot_general | solution.py:40
  225.0 0.0 all-to-all-done
  225.0 9.8 %all-to-all-start.1 = ((f32[16,24,1536]{2,1,0:T(8,128)}), f32[16,24,1536]{2,1,0:T(8,128)S(1)}, u32[]{:S(2)}, u32[]{:S(2)}) async-start(f32[16,24,1536]{2,1,0:T(8,128)} %bitcast.46), calls=%async_computation.2 | async-start | bytes 4718592 | tf_op jit(solution)/shard_map/all_to_all | solution.py:58
  234.7 3.4 slice.26
  238.2 0.8 copy.15
  238.9 0.0 copy-start.1
  238.9 2.7 copy-done.1
  241.6 1.7 convolution_bitcast_fusion.1
  243.4 47.4 %all-to-all-done.1 = f32[16,24,1536]{2,1,0:T(8,128)S(1)} async-done(((f32[16,24,1536]{2,1,0:T(8,128)}), f32[16,24,1536]{2,1,0:T(8,128)S(1)}, u32[]{:S(2)}, u32[]{:S(2)}) %all-to-all-start.1) | async-done | bytes 2359328 | tf_op jit(solution)/shard_map/all_to_all | solution.py:58
  290.8 0.1 reduce_sum.18
  290.9 9.5 %all_to_all.35 = f32[4,8,1536]{2,1,0:T(8,128)S(1)} all-to-all(f32[4,8,1536]{2,1,0:T(8,128)S(1)} %maximum_bitcast_fusion), channel_id=1, replica_groups=mesh['gx'=4,'gy'=16,'gz'=4] {'gz'}, dimensions={0} | all-to-all | bytes 393216 | tf_op jit(solution)/shard_map/all_to_all | solution.py:68
  300.4 8.7 %all_to_all.36 = f32[4,8,1536]{2,1,0:T(8,128)S(1)} all-to-all(f32[4,8,1536]{2,1,0:T(8,128)S(1)} %broadcast_in_dim.12), channel_id=1, replica_groups=mesh['gx'=4,'gy'=16,'gz'=4] {'gz'}, dimensions={0} | all-to-all | bytes 393216 | tf_op jit(solution)/shard_map/all_to_all | solution.py:71
  309.2 1.7 broadcast_in_dim.27
  310.8 0.0 slice-start
  310.8 9.3 %all-to-all-start.4 = ((f32[16,24,1536]{2,1,0:T(8,128)}), f32[16,24,1536]{2,1,0:T(8,128)}, u32[]{:S(2)}, u32[]{:S(2)}) async-start(f32[16,24,1536]{2,1,0:T(8,128)} %broadcast_in_dim.27), calls=%async_computation.5 | async-start | bytes 4718592 | tf_op jit(solution)/shard_map/all_to_all | solution.py:74
  320.1 0.0 slice-start.1
  320.1 3.9 %copy.16 = bf16[17,2,16,24,256]{4,3,2,1,0:T(8,128)(2,1)S(1)} copy(bf16[17,2,16,24,256]{4,3,1,0,2:T(8,128)(2,1)} %bitcast.7) | data formatting | bytes 13369344 | tf_op jit(solution)/shard_map/transpose | solution.py:47
  324.0 0.0 slice-done
  324.1 0.2 slice-done.1
  324.2 1.7 fusion
  326.0 11.9 %psum.7 = f32[24,384]{1,0:T(8,128)S(1)} all-reduce(f32[24,384]{1,0:T(8,128)S(1)} %reshape.65), channel_id=1, replica_groups=mesh['gx'=4,'gy'=16,'gz'=4] {'gx'}, use_global_device_ids=true, to_apply=%region_3.4 | all-reduce | flops 9216 | bytes 73728 | tf_op jit(solution)/shard_map/psum | solution.py:77
  337.9 0.6 broadcast_multiply_fusion.1
  338.5 35.0 %all-to-all-done.4 = f32[16,24,1536]{2,1,0:T(8,128)} async-done(((f32[16,24,1536]{2,1,0:T(8,128)}), f32[16,24,1536]{2,1,0:T(8,128)}, u32[]{:S(2)}, u32[]{:S(2)}) %all-to-all-start.4) | async-done | bytes 2359328 | tf_op jit(solution)/shard_map/all_to_all | solution.py:74
  373.5 3.3 broadcast_multiply_fusion
  (13 shorter events, 0.2 us)
Async XLA Ops:
  7.2 0.9 copy-start
  7.2 47.5 %reduce-scatter.2.cloned.1.call-start = ((), (), s32[]{:S(2)}) async-start(), calls=%async_computation.6 | async-start | bytes 3932160 | tf_op jit(solution)/shard_map/reduce_scatter | solution.py:21
  12.4 43.5 %copy-start.3 = (bf16[24,256]{1,0:T(8,128)(2,1)S(1)}, bf16[24,256]{1,0:T(8,128)(2,1)}, u32[]{:S(2)}) copy-start(bf16[24,256]{1,0:T(8,128)(2,1)} %param.5) | copy-start | bytes 36868
  12.4 204.8 %all-gather.2.cloned.1.call-start = ((), (), s32[]{:S(2)}) async-start(), calls=%async_computation.7 | async-start | bytes 11796480 | tf_op jit(solution)/shard_map/all_gather | solution.py:38
  59.1 158.0 %copy-start.2 = (bf16[64,2,24,384]{3,2,1,0:T(8,128)(2,1)S(1)}, bf16[64,2,24,384]{3,2,1,0:T(8,128)(2,1)}, u32[]{:S(2)}) copy-start(bf16[64,2,24,384]{3,2,1,0:T(8,128)(2,1)} %param.3) | copy-start | bytes 7077892
  59.1 165.8 %all-to-all-start = ((bf16[272,2,24,256]{3,2,1,0:T(8,128)(2,1)}), bf16[272,2,24,256]{3,2,1,0:T(8,128)(2,1)}, u32[]{:S(2)}, u32[]{:S(2)}) async-start(bf16[272,2,24,256]{3,2,1,0:T(8,128)(2,1)} %bitcast.44), calls=%async_computation.1 | async-start | bytes 13369344 | tf_op jit(solution)/shard_map/all_to_all | solution.py:36
  225.0 65.8 %all-to-all-start.1 = ((f32[16,24,1536]{2,1,0:T(8,128)}), f32[16,24,1536]{2,1,0:T(8,128)S(1)}, u32[]{:S(2)}, u32[]{:S(2)}) async-start(f32[16,24,1536]{2,1,0:T(8,128)} %bitcast.46), calls=%async_computation.2 | async-start | bytes 4718592 | tf_op jit(solution)/shard_map/all_to_all | solution.py:58
  238.9 2.7 copy-start.1
  310.8 13.2 %slice-start = ((s8[6291456]{0:T(1024)(128)(4,1)}), s8[2097152]{0:T(1024)(128)(4,1)S(1)}, s32[]{:S(2)}) async-start(s8[6291456]{0:T(1024)(128)(4,1)} %bitcast.41), calls=%async_computation.8 | async-start | bytes 4194304
  310.8 62.6 %all-to-all-start.4 = ((f32[16,24,1536]{2,1,0:T(8,128)}), f32[16,24,1536]{2,1,0:T(8,128)}, u32[]{:S(2)}, u32[]{:S(2)}) async-start(f32[16,24,1536]{2,1,0:T(8,128)} %broadcast_in_dim.27), calls=%async_computation.5 | async-start | bytes 4718592 | tf_op jit(solution)/shard_map/all_to_all | solution.py:74
  320.1 4.1 %slice-start.1 = ((s8[6291456]{0:T(1024)(128)(4,1)}), s8[4194304]{0:T(1024)(128)(4,1)S(1)}, s32[]{:S(2)}) async-start(s8[6291456]{0:T(1024)(128)(4,1)} %bitcast.41), calls=%async_computation.9 | async-start | bytes 8388608
Sparse Core Ops, SparseCore 0:
  12.5 42.1 reduce-scatter.1
  56.5 160.6 all-gather.1

commit v10 on v9

--- a/solution.py
+++ b/solution.py
@@ -18,13 +18,12 @@
     product = jnp.dot(
         field.reshape(-1, cells_one), mode_one_factor, preferred_element_type=jnp.float32
     )
-    shrunk_sum = lax.psum_scatter(
-        product.reshape(vars_all, cells_three, cells_two, rank_one),
-        "gx",
-        scatter_dimension=0,
-        tiled=True,
+    shrunk_parts = lax.all_to_all(
+        product.reshape(vars_all, cells_three, cells_two, rank_one), "gx", 0, 0, tiled=True
     )
-    field_later, shrunk_sum = lax.optimization_barrier((field, shrunk_sum))
+    shrunk_sum = jnp.sum(
+        shrunk_parts.reshape((count_gx, own_rows) + shrunk_parts.shape[1:]), axis=0
+    )
     shrunk = shrunk_sum.astype(jnp.bfloat16)
 
     if rank_one == rank_two:
@@ -35,10 +34,10 @@
     sent = jnp.broadcast_to(both[None], (count_gy,) + both.shape).reshape((-1,) + both.shape[1:])
     got = lax.all_to_all(sent, "gy", 0, 0, tiled=True).reshape((count_gy,) + both.shape)
 
-    piece = lax.all_gather(field_later, "gx", axis=3, tiled=True)
+    piece = lax.all_gather(field, "gx", axis=3, tiled=True)
     width = piece.shape[3]
     gram_block = lax.dot_general(
-        field_later.reshape(-1, cells_one),
+        field.reshape(-1, cells_one),
         piece.reshape(-1, width),
         (((0,), (0,)), ((), ())),
         preferred_element_type=jnp.float32,

time: 385 us -> 396 us (1.029)
  blocking collectives: 30.1 us -> 89.8 us
  waiting for transfers between devices: 273 us -> 227 us
    all_gather x1, waiting for transfers between devices: 149 us -> 83.1 us  [local(): piece = lax.all_gather(field, 'gx', axis=3, tiled=True)]
    all_to_all x0 -> x1, blocking collectives: none -> 59.2 us  [local(): lax.all_to_all(product.reshape(vars_all, cells_three, cells_two, rank_one...]
    all_to_all x1, waiting for transfers between devices: 0.01 us -> 58.6 us  [local(): lax.all_to_all(sent, 'gy', 0, 0, tiled=True)]
    reduce_scatter x1 -> x0, waiting for transfers between devices: 42.2 us -> none  [local(): lax.psum_scatter(product.reshape(vars_all, cells_three, cells_two, rank_o...]
  transfers between devices with their start and end apart: 5 -> 4, of which waited for: 4 -> 4; matrix products, arithmetic and copies ran while one was open for 6% -> 7% of each run, Pallas kernels for 0% -> 0%
where the time goes in v10:
time: 396 us; the launch traced here: 395 us
  waiting for transfers between devices  227 us (57%)
  blocking collectives  89.8 us (23%)
  starting transfers between devices  29 us (7%)
  local copies, waits for them, and re-layouts  16.9 us (4%)
  between operations  14.2 us (4%)
  matrix products  12.2 us (3%)
  other arithmetic  6.26 us (2%)
    all_gather x1, waiting for transfers between devices, local(): piece = lax.all_gather(field, 'gx', axis=3, tiled=True)  83.1 us
    all_to_all x1, blocking collectives, local(): lax.all_to_all(product.reshape(vars_all, cells_three, cells_two, rank_one...  59.2 us
    all_to_all x1, waiting for transfers between devices, local(): lax.all_to_all(sent, 'gy', 0, 0, tiled=True)  58.6 us
    all_to_all x1, waiting for transfers between devices, local(): parts = lax.all_to_all(gram_block, 'gy', 0, 0, tiled=True)  48.9 us
    all_to_all x1, waiting for transfers between devices, local(): gram_sum = lax.all_to_all(copies, 'gy', 0, 0, tiled=True)  35.3 us
    all_to_all x1, starting transfers between devices, local(): lax.all_to_all(sent, 'gy', 0, 0, tiled=True)  12.9 us
    psum x1, blocking collectives, local(): lax.psum(two_sum, 'gx') * (1.0 / (vars_all * total_three * rank_one))  12.1 us
    all_to_all x1, starting transfers between devices, local(): parts = lax.all_to_all(gram_block, 'gy', 0, 0, tiled=True)  9.95 us
  transfers between devices with their start and end apart: 4, of which 4 were waited for; matrix products, arithmetic and copies ran while one was open for 7% of the time, Pallas kernels for 0%

profile of v10, /device:TPU:8, one launch (start us, length us, event | category | flops | bytes accessed | tf_op | source)
XLA Modules:
  0.0 395.0 jit_solution(17183900946152163463)
XLA Ops:
  7.2 0.0 copy-start
  7.2 0.0 copy-start.2
  7.2 0.0 all-gather.2.cloned.1.call-start
  7.2 0.7 all-gather.2.cloned.1.call-update
  7.9 0.2 copy-done
  8.1 0.9 copy-done.2
  9.0 1.0 fusion.1
  9.9 59.2 %all_to_all.40 = f32[64,2,24,256]{3,2,1,0:T(8,128)S(1)} all-to-all(f32[64,2,24,256]{3,2,1,0:T(8,128)S(1)} %fusion.1), channel_id=1, replica_groups=mesh['gx'=4,'gy'=16,'gz'=4] {'gx'}, dimensions={0} | all-to-all | bytes 6291456 | tf_op jit(solution)/shard_map/all_to_all | solution.py:21
  69.1 0.0 copy-start.5
  69.1 1.1 reduce_sum.27
  70.3 0.0 copy-done.5
  70.3 1.1 pad_maximum_fusion
  71.3 3.2 broadcast_in_dim.11
  74.5 0.0 copy-start.3
  74.5 12.9 %all-to-all-start.1 = ((bf16[272,2,24,256]{3,2,1,0:T(8,128)(2,1)}), bf16[272,2,24,256]{3,2,1,0:T(8,128)(2,1)}, u32[]{:S(2)}, u32[]{:S(2)}) async-start(bf16[272,2,24,256]{3,2,1,0:T(8,128)(2,1)} %bitcast.45), calls=%async_computation.1 | async-start | bytes 13369344 | tf_op jit(solution)/shard_map/all_to_all | solution.py:35
  87.4 83.1 %all-gather.2.cloned.1.call-done = bf16[64,2,24,1536]{3,2,1,0:T(8,128)(2,1)} async-done(((bf16[64,2,24,384]{3,2,1,0:T(8,128)(2,1)}), bf16[64,2,24,1536]{3,2,1,0:T(8,128)(2,1)}) %all-gather.2.cloned.1.call-update) | async-done | bytes 9437200 | tf_op jit(solution)/shard_map/all_gather | solution.py:37
  170.5 0.0 copy-done.3
  170.5 7.8 %convolution_bitcast_fusion = f32[384,1536]{1,0:T(8,128)} fusion(bf16[64,2,24,384]{3,2,1,0:T(8,128)(2,1)S(1)} %copy-done.3, bf16[64,2,24,1536]{3,2,1,0:T(8,128)(2,1)} %all-gather.2.cloned.1.call-done), kind=kOutput, calls=%fused_computation | convolution fusion | flops 3623878656 | bytes 14155776 | tf_op jit(solution)/shard_map/dot_general | solution.py:39
  178.3 58.6 %all-to-all-done.1 = bf16[272,2,24,256]{3,2,1,0:T(8,128)(2,1)} async-done(((bf16[272,2,24,256]{3,2,1,0:T(8,128)(2,1)}), bf16[272,2,24,256]{3,2,1,0:T(8,128)(2,1)}, u32[]{:S(2)}, u32[]{:S(2)}) %all-to-all-start.1) | async-done | bytes 6684704 | tf_op jit(solution)/shard_map/all_to_all | solution.py:35
  237.0 10.0 %all-to-all-start.2 = ((f32[16,24,1536]{2,1,0:T(8,128)}), f32[16,24,1536]{2,1,0:T(8,128)S(1)}, u32[]{:S(2)}, u32[]{:S(2)}) async-start(f32[16,24,1536]{2,1,0:T(8,128)} %bitcast.48), calls=%async_computation.2 | async-start | bytes 4718592 | tf_op jit(solution)/shard_map/all_to_all | solution.py:57
  246.9 3.4 slice.26
  250.3 0.0 copy-start.4
  250.3 0.8 copy.15
  251.1 0.0 copy-start.1
  251.1 2.7 copy-done.1
  253.8 0.0 copy-done.4
  253.8 1.7 convolution_bitcast_fusion.1
  255.6 48.9 %all-to-all-done.2 = f32[16,24,1536]{2,1,0:T(8,128)S(1)} async-done(((f32[16,24,1536]{2,1,0:T(8,128)}), f32[16,24,1536]{2,1,0:T(8,128)S(1)}, u32[]{:S(2)}, u32[]{:S(2)}) %all-to-all-start.2) | async-done | bytes 2359328 | tf_op jit(solution)/shard_map/all_to_all | solution.py:57
  304.4 0.1 reduce_sum.28
  304.6 9.7 %all_to_all.41 = f32[4,8,1536]{2,1,0:T(8,128)S(1)} all-to-all(f32[4,8,1536]{2,1,0:T(8,128)S(1)} %maximum_bitcast_fusion), channel_id=1, replica_groups=mesh['gx'=4,'gy'=16,'gz'=4] {'gz'}, dimensions={0} | all-to-all | bytes 393216 | tf_op jit(solution)/shard_map/all_to_all | solution.py:67
  314.3 8.7 %all_to_all.42 = f32[4,8,1536]{2,1,0:T(8,128)S(1)} all-to-all(f32[4,8,1536]{2,1,0:T(8,128)S(1)} %broadcast_in_dim.12), channel_id=1, replica_groups=mesh['gx'=4,'gy'=16,'gz'=4] {'gz'}, dimensions={0} | all-to-all | bytes 393216 | tf_op jit(solution)/shard_map/all_to_all | solution.py:70
  323.0 1.7 broadcast_in_dim.27
  324.7 0.0 slice-start
  324.7 6.2 %all-to-all-start.5 = ((f32[16,24,1536]{2,1,0:T(8,128)}), f32[16,24,1536]{2,1,0:T(8,128)}, u32[]{:S(2)}, u32[]{:S(2)}) async-start(f32[16,24,1536]{2,1,0:T(8,128)} %broadcast_in_dim.27), calls=%async_computation.5 | async-start | bytes 4718592 | tf_op jit(solution)/shard_map/all_to_all | solution.py:73
  330.9 0.0 slice-start.1
  330.9 3.9 copy.16
  334.8 0.0 slice-done
  334.8 0.2 slice-done.1
  335.0 1.7 fusion
  336.8 12.1 %psum.7 = f32[24,384]{1,0:T(8,128)S(1)} all-reduce(f32[24,384]{1,0:T(8,128)S(1)} %reshape.69), channel_id=1, replica_groups=mesh['gx'=4,'gy'=16,'gz'=4] {'gx'}, use_global_device_ids=true, to_apply=%region_3.4 | all-reduce | flops 9216 | bytes 73728 | tf_op jit(solution)/shard_map/psum | solution.py:76
  348.9 0.6 broadcast_multiply_fusion.1
  349.5 35.3 %all-to-all-done.5 = f32[16,24,1536]{2,1,0:T(8,128)} async-done(((f32[16,24,1536]{2,1,0:T(8,128)}), f32[16,24,1536]{2,1,0:T(8,128)}, u32[]{:S(2)}, u32[]{:S(2)}) %all-to-all-start.5) | async-done | bytes 2359328 | tf_op jit(solution)/shard_map/all_to_all | solution.py:73
  384.9 3.3 broadcast_multiply_fusion
  (12 shorter events, 0.1 us)
Async XLA Ops:
  7.2 0.9 copy-start
  7.2 1.8 copy-start.2
  7.2 163.3 %all-gather.2.cloned.1.call-start = ((), (), s32[]{:S(2)}) async-start(), calls=%async_computation.6 | async-start | bytes 11796480 | tf_op jit(solution)/shard_map/all_gather | solution.py:37
  69.1 1.1 copy-start.5
  74.5 96.0 %copy-start.3 = (bf16[64,2,24,384]{3,2,1,0:T(8,128)(2,1)S(1)}, bf16[64,2,24,384]{3,2,1,0:T(8,128)(2,1)}, u32[]{:S(2)}) copy-start(bf16[64,2,24,384]{3,2,1,0:T(8,128)(2,1)} %param.3) | copy-start | bytes 7077892
  74.5 162.4 %all-to-all-start.1 = ((bf16[272,2,24,256]{3,2,1,0:T(8,128)(2,1)}), bf16[272,2,24,256]{3,2,1,0:T(8,128)(2,1)}, u32[]{:S(2)}, u32[]{:S(2)}) async-start(bf16[272,2,24,256]{3,2,1,0:T(8,128)(2,1)} %bitcast.45), calls=%async_computation.1 | async-start | bytes 13369344 | tf_op jit(solution)/shard_map/all_to_all | solution.py:35
  237.0 67.5 %all-to-all-start.2 = ((f32[16,24,1536]{2,1,0:T(8,128)}), f32[16,24,1536]{2,1,0:T(8,128)S(1)}, u32[]{:S(2)}, u32[]{:S(2)}) async-start(f32[16,24,1536]{2,1,0:T(8,128)} %bitcast.48), calls=%async_computation.2 | async-start | bytes 4718592 | tf_op jit(solution)/shard_map/all_to_all | solution.py:57
  250.3 3.5 copy-start.4
  251.1 2.7 copy-start.1
  324.7 10.1 %slice-start = ((s8[6291456]{0:T(1024)(128)(4,1)}), s8[2097152]{0:T(1024)(128)(4,1)S(1)}, s32[]{:S(2)}) async-start(s8[6291456]{0:T(1024)(128)(4,1)} %bitcast.42), calls=%async_computation.7 | async-start | bytes 4194304
  324.7 60.1 %all-to-all-start.5 = ((f32[16,24,1536]{2,1,0:T(8,128)}), f32[16,24,1536]{2,1,0:T(8,128)}, u32[]{:S(2)}, u32[]{:S(2)}) async-start(f32[16,24,1536]{2,1,0:T(8,128)} %broadcast_in_dim.27), calls=%async_computation.5 | async-start | bytes 4718592 | tf_op jit(solution)/shard_map/all_to_all | solution.py:73
  330.9 4.1 %slice-start.1 = ((s8[6291456]{0:T(1024)(128)(4,1)}), s8[4194304]{0:T(1024)(128)(4,1)S(1)}, s32[]{:S(2)}) async-start(s8[6291456]{0:T(1024)(128)(4,1)} %bitcast.42), calls=%async_computation.8 | async-start | bytes 8388608
Sparse Core Ops, SparseCore 0:
  9.8 160.6 all-gather.1

commit v11 on v7

--- a/solution.py
+++ b/solution.py
@@ -61,7 +61,11 @@
     extra_rows = -(-two_size // width)
     extra_rows = -(-extra_rows // 8) * 8
     two_rows = jnp.pad(gram_two_block.reshape(-1), (0, extra_rows * width - two_size))
-    stacked = lax.psum(jnp.concatenate([own_slice, two_rows.reshape(extra_rows, width)], axis=0), "gz")
+    stacked = jnp.concatenate([own_slice, two_rows.reshape(extra_rows, width)], axis=0)
+    count_gz = lax.axis_size("gz")
+    gz_copies = jnp.broadcast_to(stacked[None], (count_gz,) + stacked.shape).reshape(-1, width)
+    gz_blocks = lax.all_to_all(gz_copies, "gz", 0, 0, tiled=True)
+    stacked = jnp.sum(gz_blocks.reshape((count_gz,) + stacked.shape), axis=0)
     own_slice = stacked[:slice_rows]
     copies = jnp.broadcast_to(own_slice[None], (count_gy,) + own_slice.shape).reshape(-1, width)
     gram_sum = lax.all_to_all(copies, "gy", 0, 0, tiled=True)

time: 417 us -> 384 us (0.921)
  waiting for transfers between devices: 322 us -> 276 us
  blocking collectives: 11.6 us -> 26.7 us
    psum x1 -> x0, waiting for transfers between devices: 46.7 us -> none  [local(): lax.psum(jnp.concatenate([own_slice, two_rows.reshape(extra_rows, width)]...]
    all_to_all x0 -> x1, blocking collectives: none -> 15.1 us  [local(): gz_blocks = lax.all_to_all(gz_copies, 'gz', 0, 0, tiled=True)]
  transfers between devices with their start and end apart: 6 -> 5, of which waited for: 5 -> 4; matrix products, arithmetic and copies ran while one was open for 6% -> 6% of each run, Pallas kernels for 0% -> 0%
where the time goes in v11:
time: 384 us; the launch traced here: 383 us
  waiting for transfers between devices  276 us (72%)
  starting transfers between devices  28.6 us (7%)
  blocking collectives  26.7 us (7%)
  local copies, waits for them, and re-layouts  16.8 us (4%)
  matrix products  15.6 us (4%)
  between operations  14.2 us (4%)
  other arithmetic  5.3 us (1%)
    all_gather x1, waiting for transfers between devices, local(): piece = lax.all_gather(field_later, 'gx', axis=3, tiled=True)  149 us
    all_to_all x1, waiting for transfers between devices, local(): parts = lax.all_to_all(gram_block, 'gy', 0, 0, tiled=True)  47.4 us
    reduce_scatter x1, waiting for transfers between devices, local(): lax.psum_scatter(product.reshape(vars_all, cells_three, cells_two, rank_o...  42.2 us
    all_to_all x1, waiting for transfers between devices, local(): gram_sum = lax.all_to_all(copies, 'gy', 0, 0, tiled=True)  37.9 us
    all_to_all x1, blocking collectives, local(): gz_blocks = lax.all_to_all(gz_copies, 'gz', 0, 0, tiled=True)  15.1 us
    psum x1, blocking collectives, local(): lax.psum(two_sum, 'gx') * (1.0 / (vars_all * total_three * rank_one))  11.6 us
    all_to_all x1, starting transfers between devices, local(): parts = lax.all_to_all(gram_block, 'gy', 0, 0, tiled=True)  9.75 us
    all_to_all x1, starting transfers between devices, local(): lax.all_to_all(sent, 'gy', 0, 0, tiled=True)  9.41 us
  transfers between devices with their start and end apart: 5, of which 4 were waited for; matrix products, arithmetic and copies ran while one was open for 6% of the time, Pallas kernels for 0%

profile of v11, /device:TPU:8, one launch (start us, length us, event | category | flops | bytes accessed | tf_op | source)
XLA Modules:
  0.0 383.3 jit_solution(2851495070011470793)
XLA Ops:
  7.2 0.0 copy-start
  7.2 0.0 reduce-scatter.2.cloned.1.call-start
  7.2 0.9 copy-done
  8.1 4.3 %fusion.1 = f32[64,2,24,256]{3,2,1,0:T(8,128)} fusion(bf16[64,2,24,384]{3,2,1,0:T(8,128)(2,1)} %param.3, bf16[384,256]{1,0:T(8,128)(2,1)S(1)} %copy-done), kind=kOutput, calls=%fused_computation.7 | convolution fusion | flops 603979776 | bytes 5701632 | tf_op jit(solution)/shard_map/dot_general | solution.py:18
  12.4 0.0 copy-start.3
  12.4 0.0 reduce-scatter.2.cloned.1.call-update
  12.4 0.0 all-gather.2.cloned.1.call-start
  12.5 42.2 %reduce-scatter.2.cloned.1.call-done = f32[16,2,24,256]{3,2,1,0:T(8,128)} async-done(((f32[64,2,24,256]{3,2,1,0:T(8,128)}), f32[16,2,24,256]{3,2,1,0:T(8,128)}) %reduce-scatter.2.cloned.1.call-update) | async-done | bytes 786448 | tf_op jit(solution)/shard_map/reduce_scatter | solution.py:21
  54.7 0.0 all-gather.2.cloned.1.call-update
  54.7 1.2 convert_element_type.11
  55.9 0.0 copy-done.3
  56.0 3.2 broadcast_in_dim.9
  59.1 0.0 copy-start.2
  59.1 9.4 %all-to-all-start = ((bf16[272,2,24,256]{3,2,1,0:T(8,128)(2,1)}), bf16[272,2,24,256]{3,2,1,0:T(8,128)(2,1)}, u32[]{:S(2)}, u32[]{:S(2)}) async-start(bf16[272,2,24,256]{3,2,1,0:T(8,128)(2,1)} %bitcast.40), calls=%async_computation.1 | async-start | bytes 13369344 | tf_op jit(solution)/shard_map/all_to_all | solution.py:36
  68.6 148.6 %all-gather.2.cloned.1.call-done = bf16[64,2,24,1536]{3,2,1,0:T(8,128)(2,1)} async-done(((bf16[64,2,24,384]{3,2,1,0:T(8,128)(2,1)}), bf16[64,2,24,1536]{3,2,1,0:T(8,128)(2,1)}) %all-gather.2.cloned.1.call-update) | async-done | bytes 9437200 | tf_op jit(solution)/shard_map/all_gather | solution.py:38
  217.2 0.0 copy-done.2
  217.2 7.8 %convolution_bitcast_fusion = f32[384,1536]{1,0:T(8,128)} fusion(bf16[64,2,24,384]{3,2,1,0:T(8,128)(2,1)S(1)} %copy-done.2, bf16[64,2,24,1536]{3,2,1,0:T(8,128)(2,1)} %all-gather.2.cloned.1.call-done), kind=kOutput, calls=%fused_computation | convolution fusion | flops 3623878656 | bytes 14155776 | tf_op jit(solution)/shard_map/dot_general | solution.py:40
  225.0 0.0 all-to-all-done
  225.0 9.8 %all-to-all-start.1 = ((f32[16,24,1536]{2,1,0:T(8,128)}), f32[16,24,1536]{2,1,0:T(8,128)S(1)}, u32[]{:S(2)}, u32[]{:S(2)}) async-start(f32[16,24,1536]{2,1,0:T(8,128)} %bitcast.42), calls=%async_computation.2 | async-start | bytes 4718592 | tf_op jit(solution)/shard_map/all_to_all | solution.py:58
  234.7 3.4 slice.23
  238.2 0.8 copy.15
  238.9 0.0 copy-start.1
  238.9 2.7 copy-done.1
  241.6 1.7 convolution_bitcast_fusion.1
  243.4 47.4 %all-to-all-done.1 = f32[16,24,1536]{2,1,0:T(8,128)S(1)} async-done(((f32[16,24,1536]{2,1,0:T(8,128)}), f32[16,24,1536]{2,1,0:T(8,128)S(1)}, u32[]{:S(2)}, u32[]{:S(2)}) %all-to-all-start.1) | async-done | bytes 2359328 | tf_op jit(solution)/shard_map/all_to_all | solution.py:58
  290.8 0.1 reduce_sum.18
  290.9 0.1 broadcast_in_dim.10
  291.0 15.1 %all_to_all.26 = f32[4,32,1536]{2,1,0:T(8,128)S(1)} all-to-all(f32[4,32,1536]{2,1,0:T(8,128)S(1)} %broadcast_in_dim.10), channel_id=1, replica_groups=mesh['gx'=4,'gy'=16,'gz'=4] {'gz'}, dimensions={0} | all-to-all | bytes 1572864 | tf_op jit(solution)/shard_map/all_to_all | solution.py:67
  306.2 1.7 broadcast_in_dim.11
  307.9 0.0 slice-start
  307.9 9.3 %all-to-all-start.3 = ((f32[16,24,1536]{2,1,0:T(8,128)}), f32[16,24,1536]{2,1,0:T(8,128)}, u32[]{:S(2)}, u32[]{:S(2)}) async-start(f32[16,24,1536]{2,1,0:T(8,128)} %broadcast_in_dim.11), calls=%async_computation.4 | async-start | bytes 4718592 | tf_op jit(solution)/shard_map/all_to_all | solution.py:71
  317.2 0.0 slice-start.1
  317.2 3.9 %copy.16 = bf16[17,2,16,24,256]{4,3,2,1,0:T(8,128)(2,1)S(1)} copy(bf16[17,2,16,24,256]{4,3,1,0,2:T(8,128)(2,1)} %bitcast.7) | data formatting | bytes 13369344 | tf_op jit(solution)/shard_map/transpose | solution.py:47
  321.1 0.0 slice-done
  321.1 0.2 slice-done.1
  321.3 1.7 fusion
  323.1 11.6 %psum.7 = f32[24,384]{1,0:T(8,128)S(1)} all-reduce(f32[24,384]{1,0:T(8,128)S(1)} %reshape.58), channel_id=1, replica_groups=mesh['gx'=4,'gy'=16,'gz'=4] {'gx'}, use_global_device_ids=true, to_apply=%region_3.4 | all-reduce | flops 9216 | bytes 73728 | tf_op jit(solution)/shard_map/psum | solution.py:74
  334.6 0.6 broadcast_multiply_fusion.1
  335.3 37.9 %all-to-all-done.3 = f32[16,24,1536]{2,1,0:T(8,128)} async-done(((f32[16,24,1536]{2,1,0:T(8,128)}), f32[16,24,1536]{2,1,0:T(8,128)}, u32[]{:S(2)}, u32[]{:S(2)}) %all-to-all-start.3) | async-done | bytes 2359328 | tf_op jit(solution)/shard_map/all_to_all | solution.py:71
  373.2 3.3 broadcast_multiply_fusion
  (12 shorter events, 0.2 us)
Async XLA Ops:
  7.2 0.9 copy-start
  7.2 47.5 %reduce-scatter.2.cloned.1.call-start = ((), (), s32[]{:S(2)}) async-start(), calls=%async_computation.5 | async-start | bytes 3932160 | tf_op jit(solution)/shard_map/reduce_scatter | solution.py:21
  12.4 43.5 %copy-start.3 = (bf16[24,256]{1,0:T(8,128)(2,1)S(1)}, bf16[24,256]{1,0:T(8,128)(2,1)}, u32[]{:S(2)}) copy-start(bf16[24,256]{1,0:T(8,128)(2,1)} %param.5) | copy-start | bytes 36868
  12.4 204.8 %all-gather.2.cloned.1.call-start = ((), (), s32[]{:S(2)}) async-start(), calls=%async_computation.6 | async-start | bytes 11796480 | tf_op jit(solution)/shard_map/all_gather | solution.py:38
  59.1 158.0 %copy-start.2 = (bf16[64,2,24,384]{3,2,1,0:T(8,128)(2,1)S(1)}, bf16[64,2,24,384]{3,2,1,0:T(8,128)(2,1)}, u32[]{:S(2)}) copy-start(bf16[64,2,24,384]{3,2,1,0:T(8,128)(2,1)} %param.3) | copy-start | bytes 7077892
  59.1 165.8 %all-to-all-start = ((bf16[272,2,24,256]{3,2,1,0:T(8,128)(2,1)}), bf16[272,2,24,256]{3,2,1,0:T(8,128)(2,1)}, u32[]{:S(2)}, u32[]{:S(2)}) async-start(bf16[272,2,24,256]{3,2,1,0:T(8,128)(2,1)} %bitcast.40), calls=%async_computation.1 | async-start | bytes 13369344 | tf_op jit(solution)/shard_map/all_to_all | solution.py:36
  225.0 65.8 %all-to-all-start.1 = ((f32[16,24,1536]{2,1,0:T(8,128)}), f32[16,24,1536]{2,1,0:T(8,128)S(1)}, u32[]{:S(2)}, u32[]{:S(2)}) async-start(f32[16,24,1536]{2,1,0:T(8,128)} %bitcast.42), calls=%async_computation.2 | async-start | bytes 4718592 | tf_op jit(solution)/shard_map/all_to_all | solution.py:58
  238.9 2.7 copy-start.1
  307.9 13.3 %slice-start = ((s8[6291456]{0:T(1024)(128)(4,1)}), s8[2097152]{0:T(1024)(128)(4,1)S(1)}, s32[]{:S(2)}) async-start(s8[6291456]{0:T(1024)(128)(4,1)} %bitcast.37), calls=%async_computation.7 | async-start | bytes 4194304
  307.9 65.3 %all-to-all-start.3 = ((f32[16,24,1536]{2,1,0:T(8,128)}), f32[16,24,1536]{2,1,0:T(8,128)}, u32[]{:S(2)}, u32[]{:S(2)}) async-start(f32[16,24,1536]{2,1,0:T(8,128)} %broadcast_in_dim.11), calls=%async_computation.4 | async-start | bytes 4718592 | tf_op jit(solution)/shard_map/all_to_all | solution.py:71
  317.2 4.1 %slice-start.1 = ((s8[6291456]{0:T(1024)(128)(4,1)}), s8[4194304]{0:T(1024)(128)(4,1)S(1)}, s32[]{:S(2)}) async-start(s8[6291456]{0:T(1024)(128)(4,1)} %bitcast.37), calls=%async_computation.8 | async-start | bytes 8388608
Sparse Core Ops, SparseCore 0:
  12.5 42.1 reduce-scatter.1
  56.5 160.6 all-gather.1

commit v12 on v11

--- a/solution.py
+++ b/solution.py
@@ -55,8 +55,8 @@
     )
 
     slice_rows = gram_block.shape[0] // count_gy
-    parts = lax.all_to_all(gram_block, "gy", 0, 0, tiled=True)
-    own_slice = jnp.sum(parts.reshape(count_gy, slice_rows, width), axis=0)
+    parts = lax.all_to_all(gram_block.astype(jnp.bfloat16), "gy", 0, 0, tiled=True)
+    own_slice = jnp.sum(parts.reshape(count_gy, slice_rows, width).astype(jnp.float32), axis=0)
     two_size = gram_two_block.size
     extra_rows = -(-two_size // width)
     extra_rows = -(-extra_rows // 8) * 8

time: 384 us -> 357 us (0.930)
  waiting for transfers between devices: 276 us -> 253 us
    all_to_all x1, waiting for transfers between devices: 47.4 us -> 23.9 us  [local(): lax.all_to_all(gram_block.astype(jnp.bfloat16), 'gy', 0, 0, tiled=True)]
where the time goes in v12:
time: 357 us; the launch traced here: 356 us
  waiting for transfers between devices  253 us (71%)
  blocking collectives  26.1 us (7%)
  starting transfers between devices  25 us (7%)
  local copies, waits for them, and re-layouts  17.9 us (5%)
  matrix products  15.3 us (4%)
  between operations  14.2 us (4%)
  other arithmetic  4.21 us (1%)
    all_gather x1, waiting for transfers between devices, local(): piece = lax.all_gather(field_later, 'gx', axis=3, tiled=True)  149 us
    reduce_scatter x1, waiting for transfers between devices, local(): lax.psum_scatter(product.reshape(vars_all, cells_three, cells_two, rank_o...  42.2 us
    all_to_all x1, waiting for transfers between devices, local(): gram_sum = lax.all_to_all(copies, 'gy', 0, 0, tiled=True)  38.1 us
    all_to_all x1, waiting for transfers between devices, local(): lax.all_to_all(gram_block.astype(jnp.bfloat16), 'gy', 0, 0, tiled=True)  23.9 us
    all_to_all x1, blocking collectives, local(): gz_blocks = lax.all_to_all(gz_copies, 'gz', 0, 0, tiled=True)  14.6 us
    psum x1, blocking collectives, local(): lax.psum(two_sum, 'gx') * (1.0 / (vars_all * total_three * rank_one))  11.6 us
    all_to_all x1, starting transfers between devices, local(): lax.all_to_all(gram_block.astype(jnp.bfloat16), 'gy', 0, 0, tiled=True)  9.76 us
    all_to_all x1, starting transfers between devices, local(): lax.all_to_all(sent, 'gy', 0, 0, tiled=True)  9.41 us
  transfers between devices with their start and end apart: 5, of which 4 were waited for; matrix products, arithmetic and copies ran while one was open for 6% of the time, Pallas kernels for 0%

profile of v12, /device:TPU:8, one launch (start us, length us, event | category | flops | bytes accessed | tf_op | source)
XLA Modules:
  0.0 355.6 jit_solution(5536436144476743032)
XLA Ops:
  7.2 0.0 copy-start
  7.2 0.0 reduce-scatter.2.cloned.1.call-start
  7.2 0.9 copy-done
  8.1 4.3 %fusion.1 = f32[64,2,24,256]{3,2,1,0:T(8,128)} fusion(bf16[64,2,24,384]{3,2,1,0:T(8,128)(2,1)} %param.3, bf16[384,256]{1,0:T(8,128)(2,1)S(1)} %copy-done), kind=kOutput, calls=%fused_computation.8 | convolution fusion | flops 603979776 | bytes 5701632 | tf_op jit(solution)/shard_map/dot_general | solution.py:18
  12.4 0.0 reduce-scatter.2.cloned.1.call-update
  12.4 0.0 copy-start.4
  12.4 0.0 all-gather.2.cloned.1.call-start
  12.5 42.2 %reduce-scatter.2.cloned.1.call-done = f32[16,2,24,256]{3,2,1,0:T(8,128)} async-done(((f32[64,2,24,256]{3,2,1,0:T(8,128)}), f32[16,2,24,256]{3,2,1,0:T(8,128)}) %reduce-scatter.2.cloned.1.call-update) | async-done | bytes 786448 | tf_op jit(solution)/shard_map/reduce_scatter | solution.py:21
  54.7 0.0 copy-start.3
  54.7 0.0 all-gather.2.cloned.1.call-update
  54.7 1.1 copy-done.3
  55.9 0.0 copy-done.4
  55.9 3.2 broadcast_in_dim.9
  59.1 0.0 copy-start.2
  59.1 9.4 %all-to-all-start = ((bf16[272,2,24,256]{3,2,1,0:T(8,128)(2,1)}), bf16[272,2,24,256]{3,2,1,0:T(8,128)(2,1)}, u32[]{:S(2)}, u32[]{:S(2)}) async-start(bf16[272,2,24,256]{3,2,1,0:T(8,128)(2,1)} %bitcast.40), calls=%async_computation.1 | async-start | bytes 13369344 | tf_op jit(solution)/shard_map/all_to_all | solution.py:36
  68.5 148.6 %all-gather.2.cloned.1.call-done = bf16[64,2,24,1536]{3,2,1,0:T(8,128)(2,1)} async-done(((bf16[64,2,24,384]{3,2,1,0:T(8,128)(2,1)}), bf16[64,2,24,1536]{3,2,1,0:T(8,128)(2,1)}) %all-gather.2.cloned.1.call-update) | async-done | bytes 9437200 | tf_op jit(solution)/shard_map/all_gather | solution.py:38
  217.1 0.0 copy-done.2
  217.1 7.5 %convolution_bitcast_fusion = bf16[384,1536]{1,0:T(8,128)(2,1)} fusion(bf16[64,2,24,384]{3,2,1,0:T(8,128)(2,1)S(1)} %copy-done.2, bf16[64,2,24,1536]{3,2,1,0:T(8,128)(2,1)} %all-gather.2.cloned.1.call-done), kind=kOutput, calls=%fused_computation | convolution fusion | flops 3623878656 | bytes 12976128 | tf_op jit(solution)/shard_map/dot_general | solution.py:40
  224.7 0.0 all-to-all-done
  224.7 9.8 %all-to-all-start.1 = ((bf16[16,24,1536]{2,1,0:T(8,128)(2,1)}), bf16[16,24,1536]{2,1,0:T(8,128)(2,1)S(1)}, u32[]{:S(2)}, u32[]{:S(2)}) async-start(bf16[16,24,1536]{2,1,0:T(8,128)(2,1)} %bitcast.43), calls=%async_computation.2 | async-start | bytes 2359296 | tf_op jit(solution)/shard_map/all_to_all | solution.py:58
  234.4 3.4 slice.23
  237.9 0.8 copy.15
  238.6 0.0 copy-start.1
  238.7 2.7 copy-done.1
  241.3 1.7 convolution_bitcast_fusion.1
  243.1 23.9 %all-to-all-done.1 = bf16[16,24,1536]{2,1,0:T(8,128)(2,1)S(1)} async-done(((bf16[16,24,1536]{2,1,0:T(8,128)(2,1)}), bf16[16,24,1536]{2,1,0:T(8,128)(2,1)S(1)}, u32[]{:S(2)}, u32[]{:S(2)}) %all-to-all-start.1) | async-done | bytes 1179680 | tf_op jit(solution)/shard_map/all_to_all | solution.py:58
  267.0 0.2 convert_reduce_fusion
  267.2 0.1 broadcast_in_dim.10
  267.2 14.6 %all_to_all.26 = f32[4,32,1536]{2,1,0:T(8,128)S(1)} all-to-all(f32[4,32,1536]{2,1,0:T(8,128)S(1)} %broadcast_in_dim.10), channel_id=1, replica_groups=mesh['gx'=4,'gy'=16,'gz'=4] {'gz'}, dimensions={0} | all-to-all | bytes 1572864 | tf_op jit(solution)/shard_map/all_to_all | solution.py:67
  281.9 1.7 broadcast_in_dim.11
  283.5 0.0 slice-start
  283.5 5.8 %all-to-all-start.3 = ((f32[16,24,1536]{2,1,0:T(8,128)}), f32[16,24,1536]{2,1,0:T(8,128)}, u32[]{:S(2)}, u32[]{:S(2)}) async-start(f32[16,24,1536]{2,1,0:T(8,128)} %broadcast_in_dim.11), calls=%async_computation.4 | async-start | bytes 4718592 | tf_op jit(solution)/shard_map/all_to_all | solution.py:71
  289.3 0.0 slice-start.1
  289.3 3.9 %copy.16 = bf16[17,2,16,24,256]{4,3,2,1,0:T(8,128)(2,1)S(1)} copy(bf16[17,2,16,24,256]{4,3,1,0,2:T(8,128)(2,1)} %bitcast.7) | data formatting | bytes 13369344 | tf_op jit(solution)/shard_map/transpose | solution.py:47
  293.2 0.0 slice-done
  293.3 0.2 slice-done.1
  293.4 1.7 fusion
  295.2 11.6 %psum.7 = f32[24,384]{1,0:T(8,128)S(1)} all-reduce(f32[24,384]{1,0:T(8,128)S(1)} %reshape.58), channel_id=1, replica_groups=mesh['gx'=4,'gy'=16,'gz'=4] {'gx'}, use_global_device_ids=true, to_apply=%region_3.4 | all-reduce | flops 9216 | bytes 73728 | tf_op jit(solution)/shard_map/psum | solution.py:74
  306.8 0.6 broadcast_multiply_fusion.1
  307.4 38.1 %all-to-all-done.3 = f32[16,24,1536]{2,1,0:T(8,128)} async-done(((f32[16,24,1536]{2,1,0:T(8,128)}), f32[16,24,1536]{2,1,0:T(8,128)}, u32[]{:S(2)}, u32[]{:S(2)}) %all-to-all-start.3) | async-done | bytes 2359328 | tf_op jit(solution)/shard_map/all_to_all | solution.py:71
  345.5 3.3 broadcast_multiply_fusion
  (13 shorter events, 0.2 us)
Async XLA Ops:
  7.2 0.9 copy-start
  7.2 47.5 %reduce-scatter.2.cloned.1.call-start = ((), (), s32[]{:S(2)}) async-start(), calls=%async_computation.5 | async-start | bytes 3932160 | tf_op jit(solution)/shard_map/reduce_scatter | solution.py:21
  12.4 43.5 %copy-start.4 = (bf16[24,256]{1,0:T(8,128)(2,1)S(1)}, bf16[24,256]{1,0:T(8,128)(2,1)}, u32[]{:S(2)}) copy-start(bf16[24,256]{1,0:T(8,128)(2,1)} %param.5) | copy-start | bytes 36868
  12.4 204.7 %all-gather.2.cloned.1.call-start = ((), (), s32[]{:S(2)}) async-start(), calls=%async_computation.6 | async-start | bytes 11796480 | tf_op jit(solution)/shard_map/all_gather | solution.py:38
  54.7 1.1 copy-start.3
  59.1 158.0 %copy-start.2 = (bf16[64,2,24,384]{3,2,1,0:T(8,128)(2,1)S(1)}, bf16[64,2,24,384]{3,2,1,0:T(8,128)(2,1)}, u32[]{:S(2)}) copy-start(bf16[64,2,24,384]{3,2,1,0:T(8,128)(2,1)} %param.3) | copy-start | bytes 7077892
  59.1 165.6 %all-to-all-start = ((bf16[272,2,24,256]{3,2,1,0:T(8,128)(2,1)}), bf16[272,2,24,256]{3,2,1,0:T(8,128)(2,1)}, u32[]{:S(2)}, u32[]{:S(2)}) async-start(bf16[272,2,24,256]{3,2,1,0:T(8,128)(2,1)} %bitcast.40), calls=%async_computation.1 | async-start | bytes 13369344 | tf_op jit(solution)/shard_map/all_to_all | solution.py:36
  224.7 42.3 %all-to-all-start.1 = ((bf16[16,24,1536]{2,1,0:T(8,128)(2,1)}), bf16[16,24,1536]{2,1,0:T(8,128)(2,1)S(1)}, u32[]{:S(2)}, u32[]{:S(2)}) async-start(bf16[16,24,1536]{2,1,0:T(8,128)(2,1)} %bitcast.43), calls=%async_computation.2 | async-start | bytes 2359296 | tf_op jit(solution)/shard_map/all_to_all | solution.py:58
  238.6 2.7 copy-start.1
  283.5 9.7 %slice-start = ((s8[6291456]{0:T(1024)(128)(4,1)}), s8[2097152]{0:T(1024)(128)(4,1)S(1)}, s32[]{:S(2)}) async-start(s8[6291456]{0:T(1024)(128)(4,1)} %bitcast.37), calls=%async_computation.7 | async-start | bytes 4194304
  283.5 61.9 %all-to-all-start.3 = ((f32[16,24,1536]{2,1,0:T(8,128)}), f32[16,24,1536]{2,1,0:T(8,128)}, u32[]{:S(2)}, u32[]{:S(2)}) async-start(f32[16,24,1536]{2,1,0:T(8,128)} %broadcast_in_dim.11), calls=%async_computation.4 | async-start | bytes 4718592 | tf_op jit(solution)/shard_map/all_to_all | solution.py:71
  289.3 4.1 %slice-start.1 = ((s8[6291456]{0:T(1024)(128)(4,1)}), s8[4194304]{0:T(1024)(128)(4,1)S(1)}, s32[]{:S(2)}) async-start(s8[6291456]{0:T(1024)(128)(4,1)} %bitcast.37), calls=%async_computation.8 | async-start | bytes 8388608
Sparse Core Ops, SparseCore 0:
  12.5 42.1 reduce-scatter.1
  56.5 160.5 all-gather.1

commit v13 on v12

--- a/solution.py
+++ b/solution.py
@@ -68,7 +68,7 @@
     stacked = jnp.sum(gz_blocks.reshape((count_gz,) + stacked.shape), axis=0)
     own_slice = stacked[:slice_rows]
     copies = jnp.broadcast_to(own_slice[None], (count_gy,) + own_slice.shape).reshape(-1, width)
-    gram_sum = lax.all_to_all(copies, "gy", 0, 0, tiled=True)
+    gram_sum = lax.all_to_all(copies.astype(jnp.bfloat16), "gy", 0, 0, tiled=True).astype(jnp.float32)
     gram_one = gram_sum * (1.0 / (vars_all * total_three * total_two))
     two_sum = stacked[slice_rows:].reshape(-1)[:two_size].reshape(gram_two_block.shape)
     gram_two = lax.psum(two_sum, "gx") * (1.0 / (vars_all * total_three * rank_one))

time: 357 us -> 329 us (0.922)
  waiting for transfers between devices: 253 us -> 226 us
    all_to_all x1, waiting for transfers between devices: 38.1 us -> 11.6 us  [local(): lax.all_to_all(copies.astype(jnp.bfloat16), 'gy', 0, 0, tiled=True)]
  transfers between devices with their start and end apart: 5 -> 5, of which waited for: 4 -> 4; matrix products, arithmetic and copies ran while one was open for 6% -> 7% of each run, Pallas kernels for 0% -> 0%
where the time goes in v13:
time: 329 us; the launch traced here: 327 us
  waiting for transfers between devices  226 us (69%)
  starting transfers between devices  26.3 us (8%)
  blocking collectives  24.5 us (7%)
  local copies, waits for them, and re-layouts  18 us (5%)
  matrix products  15.3 us (5%)
  between operations  14.2 us (4%)
    all_gather x1, waiting for transfers between devices, local(): piece = lax.all_gather(field_later, 'gx', axis=3, tiled=True)  149 us
    reduce_scatter x1, waiting for transfers between devices, local(): lax.psum_scatter(product.reshape(vars_all, cells_three, cells_two, rank_o...  42.2 us
    all_to_all x1, waiting for transfers between devices, local(): lax.all_to_all(gram_block.astype(jnp.bfloat16), 'gy', 0, 0, tiled=True)  24.1 us
    all_to_all x1, blocking collectives, local(): gz_blocks = lax.all_to_all(gz_copies, 'gz', 0, 0, tiled=True)  13.1 us
    all_to_all x1, waiting for transfers between devices, local(): lax.all_to_all(copies.astype(jnp.bfloat16), 'gy', 0, 0, tiled=True)  11.6 us
    psum x1, blocking collectives, local(): lax.psum(two_sum, 'gx') * (1.0 / (vars_all * total_three * rank_one))  11.4 us
    all_to_all x1, starting transfers between devices, local(): lax.all_to_all(gram_block.astype(jnp.bfloat16), 'gy', 0, 0, tiled=True)  9.76 us
    all_to_all x1, starting transfers between devices, local(): lax.all_to_all(sent, 'gy', 0, 0, tiled=True)  9.41 us
  transfers between devices with their start and end apart: 5, of which 4 were waited for; matrix products, arithmetic and copies ran while one was open for 7% of the time, Pallas kernels for 0%

profile of v13, /device:TPU:8, one launch (start us, length us, event | category | flops | bytes accessed | tf_op | source)
XLA Modules:
  0.0 327.4 jit_solution(5315135300613165793)
XLA Ops:
  7.2 0.0 copy-start
  7.2 0.0 reduce-scatter.2.cloned.1.call-start
  7.2 0.9 copy-done
  8.1 4.3 %fusion.1 = f32[64,2,24,256]{3,2,1,0:T(8,128)} fusion(bf16[64,2,24,384]{3,2,1,0:T(8,128)(2,1)} %param.3, bf16[384,256]{1,0:T(8,128)(2,1)S(1)} %copy-done), kind=kOutput, calls=%fused_computation.8 | convolution fusion | flops 603979776 | bytes 5701632 | tf_op jit(solution)/shard_map/dot_general | solution.py:18
  12.4 0.0 reduce-scatter.2.cloned.1.call-update
  12.4 0.0 copy-start.5
  12.4 0.0 all-gather.2.cloned.1.call-start
  12.5 42.2 %reduce-scatter.2.cloned.1.call-done = f32[16,2,24,256]{3,2,1,0:T(8,128)} async-done(((f32[64,2,24,256]{3,2,1,0:T(8,128)}), f32[16,2,24,256]{3,2,1,0:T(8,128)}) %reduce-scatter.2.cloned.1.call-update) | async-done | bytes 786448 | tf_op jit(solution)/shard_map/reduce_scatter | solution.py:21
  54.7 0.0 copy-start.3
  54.7 0.0 all-gather.2.cloned.1.call-update
  54.7 1.1 copy-done.3
  55.8 0.0 copy-done.5
  55.9 3.2 broadcast_in_dim.9
  59.1 0.0 copy-start.2
  59.1 9.4 %all-to-all-start = ((bf16[272,2,24,256]{3,2,1,0:T(8,128)(2,1)}), bf16[272,2,24,256]{3,2,1,0:T(8,128)(2,1)}, u32[]{:S(2)}, u32[]{:S(2)}) async-start(bf16[272,2,24,256]{3,2,1,0:T(8,128)(2,1)} %bitcast.40), calls=%async_computation.1 | async-start | bytes 13369344 | tf_op jit(solution)/shard_map/all_to_all | solution.py:36
  68.5 148.6 %all-gather.2.cloned.1.call-done = bf16[64,2,24,1536]{3,2,1,0:T(8,128)(2,1)} async-done(((bf16[64,2,24,384]{3,2,1,0:T(8,128)(2,1)}), bf16[64,2,24,1536]{3,2,1,0:T(8,128)(2,1)}) %all-gather.2.cloned.1.call-update) | async-done | bytes 9437200 | tf_op jit(solution)/shard_map/all_gather | solution.py:38
  217.1 0.0 copy-done.2
  217.1 7.5 %convolution_bitcast_fusion = bf16[384,1536]{1,0:T(8,128)(2,1)} fusion(bf16[64,2,24,384]{3,2,1,0:T(8,128)(2,1)S(1)} %copy-done.2, bf16[64,2,24,1536]{3,2,1,0:T(8,128)(2,1)} %all-gather.2.cloned.1.call-done), kind=kOutput, calls=%fused_computation | convolution fusion | flops 3623878656 | bytes 12976128 | tf_op jit(solution)/shard_map/dot_general | solution.py:40
  224.7 0.0 all-to-all-done
  224.7 9.8 %all-to-all-start.1 = ((bf16[16,24,1536]{2,1,0:T(8,128)(2,1)}), bf16[16,24,1536]{2,1,0:T(8,128)(2,1)S(1)}, u32[]{:S(2)}, u32[]{:S(2)}) async-start(bf16[16,24,1536]{2,1,0:T(8,128)(2,1)} %bitcast.43), calls=%async_computation.2 | async-start | bytes 2359296 | tf_op jit(solution)/shard_map/all_to_all | solution.py:58
  234.5 3.4 %slice.24 = bf16[16,2,16,24,256]{4,3,1,0,2:T(8,128)(2,1)S(1)} slice(bf16[17,2,16,24,256]{4,3,1,0,2:T(8,128)(2,1)} %bitcast.7), slice={[0:16], [0:2], [0:16], [0:24], [0:256]} | slice | bytes 12582912 | tf_op jit(solution)/shard_map/slice | solution.py:48
  237.9 0.8 copy.15
  238.6 0.0 copy-start.1
  238.7 2.6 copy-done.1
  241.3 1.7 convolution_bitcast_fusion.1
  243.1 24.1 %all-to-all-done.1 = bf16[16,24,1536]{2,1,0:T(8,128)(2,1)S(1)} async-done(((bf16[16,24,1536]{2,1,0:T(8,128)(2,1)}), bf16[16,24,1536]{2,1,0:T(8,128)(2,1)S(1)}, u32[]{:S(2)}, u32[]{:S(2)}) %all-to-all-start.1) | async-done | bytes 1179680 | tf_op jit(solution)/shard_map/all_to_all | solution.py:58
  267.1 0.2 convert_reduce_fusion
  267.3 0.1 broadcast_in_dim.10
  267.4 13.1 %all_to_all.26 = f32[4,32,1536]{2,1,0:T(8,128)S(1)} all-to-all(f32[4,32,1536]{2,1,0:T(8,128)S(1)} %broadcast_in_dim.10), channel_id=1, replica_groups=mesh['gx'=4,'gy'=16,'gz'=4] {'gz'}, dimensions={0} | all-to-all | bytes 1572864 | tf_op jit(solution)/shard_map/all_to_all | solution.py:67
  280.6 0.0 copy-start.4
  280.6 0.6 copy-done.4
  281.2 1.1 broadcast_in_dim.11
  282.3 0.0 slice-start
  282.3 7.0 %all-to-all-start.3 = ((bf16[16,24,1536]{2,1,0:T(8,128)(2,1)}), bf16[16,24,1536]{2,1,0:T(8,128)(2,1)S(1)}, u32[]{:S(2)}, u32[]{:S(2)}) async-start(bf16[16,24,1536]{2,1,0:T(8,128)(2,1)} %broadcast_in_dim.11), calls=%async_computation.4 | async-start | bytes 2359296 | tf_op jit(solution)/shard_map/all_to_all | solution.py:71
  289.4 0.0 slice-start.1
  289.4 3.9 %copy.16 = bf16[17,2,16,24,256]{4,3,2,1,0:T(8,128)(2,1)S(1)} copy(bf16[17,2,16,24,256]{4,3,1,0,2:T(8,128)(2,1)} %bitcast.7) | data formatting | bytes 13369344 | tf_op jit(solution)/shard_map/transpose | solution.py:47
  293.3 0.0 slice-done
  293.3 0.2 slice-done.1
  293.5 0.0 slice-start.2
  293.5 1.7 fusion
  295.2 0.0 slice-done.2
  295.2 11.4 %psum.7 = f32[24,384]{1,0:T(8,128)S(1)} all-reduce(f32[24,384]{1,0:T(8,128)S(1)} %reshape.58), channel_id=1, replica_groups=mesh['gx'=4,'gy'=16,'gz'=4] {'gx'}, use_global_device_ids=true, to_apply=%region_3.4 | all-reduce | flops 9216 | bytes 73728 | tf_op jit(solution)/shard_map/psum | solution.py:74
  306.6 0.6 broadcast_multiply_fusion
  307.2 11.6 %all-to-all-done.3 = bf16[16,24,1536]{2,1,0:T(8,128)(2,1)S(1)} async-done(((bf16[16,24,1536]{2,1,0:T(8,128)(2,1)}), bf16[16,24,1536]{2,1,0:T(8,128)(2,1)S(1)}, u32[]{:S(2)}, u32[]{:S(2)}) %all-to-all-start.3) | async-done | bytes 1179680 | tf_op jit(solution)/shard_map/all_to_all | solution.py:71
  318.8 1.7 convert_multiply_fusion
  (12 shorter events, 0.2 us)
Async XLA Ops:
  7.2 0.9 copy-start
  7.2 47.5 %reduce-scatter.2.cloned.1.call-start = ((), (), s32[]{:S(2)}) async-start(), calls=%async_computation.5 | async-start | bytes 3932160 | tf_op jit(solution)/shard_map/reduce_scatter | solution.py:21
  12.4 43.5 %copy-start.5 = (bf16[24,256]{1,0:T(8,128)(2,1)S(1)}, bf16[24,256]{1,0:T(8,128)(2,1)}, u32[]{:S(2)}) copy-start(bf16[24,256]{1,0:T(8,128)(2,1)} %param.5) | copy-start | bytes 36868
  12.4 204.7 %all-gather.2.cloned.1.call-start = ((), (), s32[]{:S(2)}) async-start(), calls=%async_computation.6 | async-start | bytes 11796480 | tf_op jit(solution)/shard_map/all_gather | solution.py:38
  54.7 1.1 copy-start.3
  59.1 158.0 %copy-start.2 = (bf16[64,2,24,384]{3,2,1,0:T(8,128)(2,1)S(1)}, bf16[64,2,24,384]{3,2,1,0:T(8,128)(2,1)}, u32[]{:S(2)}) copy-start(bf16[64,2,24,384]{3,2,1,0:T(8,128)(2,1)} %param.3) | copy-start | bytes 7077892
  59.1 165.6 %all-to-all-start = ((bf16[272,2,24,256]{3,2,1,0:T(8,128)(2,1)}), bf16[272,2,24,256]{3,2,1,0:T(8,128)(2,1)}, u32[]{:S(2)}, u32[]{:S(2)}) async-start(bf16[272,2,24,256]{3,2,1,0:T(8,128)(2,1)} %bitcast.40), calls=%async_computation.1 | async-start | bytes 13369344 | tf_op jit(solution)/shard_map/all_to_all | solution.py:36
  224.7 42.5 %all-to-all-start.1 = ((bf16[16,24,1536]{2,1,0:T(8,128)(2,1)}), bf16[16,24,1536]{2,1,0:T(8,128)(2,1)S(1)}, u32[]{:S(2)}, u32[]{:S(2)}) async-start(bf16[16,24,1536]{2,1,0:T(8,128)(2,1)} %bitcast.43), calls=%async_computation.2 | async-start | bytes 2359296 | tf_op jit(solution)/shard_map/all_to_all | solution.py:58
  238.6 2.7 copy-start.1
  280.6 0.7 copy-start.4
  282.3 10.9 %slice-start = ((s8[6291456]{0:T(1024)(128)(4,1)}), s8[2097152]{0:T(1024)(128)(4,1)S(1)}, s32[]{:S(2)}) async-start(s8[6291456]{0:T(1024)(128)(4,1)} %bitcast.37), calls=%async_computation.7 | async-start | bytes 4194304
  282.3 36.5 %all-to-all-start.3 = ((bf16[16,24,1536]{2,1,0:T(8,128)(2,1)}), bf16[16,24,1536]{2,1,0:T(8,128)(2,1)S(1)}, u32[]{:S(2)}, u32[]{:S(2)}) async-start(bf16[16,24,1536]{2,1,0:T(8,128)(2,1)} %broadcast_in_dim.11), calls=%async_computation.4 | async-start | bytes 2359296 | tf_op jit(solution)/shard_map/all_to_all | solution.py:71
  289.4 4.1 %slice-start.1 = ((s8[6291456]{0:T(1024)(128)(4,1)}), s8[4194304]{0:T(1024)(128)(4,1)S(1)}, s32[]{:S(2)}) async-start(s8[6291456]{0:T(1024)(128)(4,1)} %bitcast.37), calls=%async_computation.8 | async-start | bytes 8388608
  293.5 1.7 slice-start.2
Sparse Core Ops, SparseCore 0:
  12.5 42.1 reduce-scatter.1
  56.5 160.5 all-gather.1
